TPU v7x, 512 devices: a whole 4x8x8 slice. The times are simulated.
512 devices in a mesh: seq: 32 (over x, z), head: 16 (over y, core).
Axes of the slice: x: 4, y: 8, z: 8, core: 2. Of those that a mesh axis runs over, the one named last changes fastest.
Arguments:
- inputs: bfloat16 [32768, 8192], P('seq', 'head'), may hold values from -6 to 6
- in_map: bfloat16 [32768, 128], P('seq'), may hold values from -1.25 to 1.25
- out_map: bfloat16 [32768, 128], P('seq'), may hold values from -1.25 to 1.25
- log_decay: float32 [64, 32768], P('head', 'seq'), may hold values from -0.8 to 0, as said below
- cotangent: bfloat16 [32768, 8192], P('seq', 'head'), may hold values from -0.4375 to 0.4375
Outputs:
- grad_inputs: float32 [32768, 8192], P('seq', 'head')
- grad_in_map: float32 [32768, 128], P(('seq', 'head'))
- grad_out_map: float32 [32768, 128], P(('seq', 'head'))
- grad_decay: float32 [64, 32768], P('head', 'seq')
Inputs may be any that keep to these rules, and one draw needn't show every extreme that they name: `log_decay`: entries are negative.
All inputs are finite; a program needn't handle non-finite values.
Results may differ from a plain program's by a relative error of at most 0.00035.
Values sent between devices are 32-bit elements; how exact they have to be, the bound alone decides.
No kernel may reach another device: no remote copies, remote signals or barrier semaphores. Data moves between devices by JAX's collectives and lax.ppermute only.
A program may use at most 128 MiB of HBM per device.

v0:
```python
import jax
import jax.numpy as jnp
from jax import lax
from jax.sharding import PartitionSpec as P

BLOCK = 512


highest = lax.Precision.HIGHEST


def prefix(array, axis, combine, identity, reverse):
    peers, mine = (lax.axis_size(axis), lax.axis_index(axis))
    everything = jax.tree.map(lambda part: lax.all_gather(part, axis), array)
    start = jax.tree.map(
        lambda part, zero: jnp.broadcast_to(jnp.asarray(zero, part.dtype), part.shape),
        array,
        identity,
    )

    def hop(k, before):
        at = peers - 1 - k if reverse else k
        reached = at > mine if reverse else at < mine
        new = combine(before, jax.tree.map(lambda part: part[at], everything))
        return jax.tree.map(lambda a, b: jnp.where(reached, a, b), new, before)

    return lax.fori_loop(0, peers, hop, start)


def triangles(length):
    locations = jnp.arange(length)
    upper = (locations[:, None] <= locations[None, :]).astype(jnp.float32)
    return (upper, upper.T)


def local_block(pieces):
    inputs_blk, in_blk, out_blk, rates, cotan_blk = pieces
    upper, lower = triangles(rates.shape[1])
    running = jnp.dot(rates, upper, precision=highest)
    causal = lower[None] > 0
    gaps = running[:, :, None] - running[:, None, :]
    decays = jnp.where(causal, jnp.exp(jnp.where(causal, gaps, 0.0)), 0.0)
    scores = jnp.dot(out_blk, in_blk.T, preferred_element_type=jnp.float32)
    pairs = jnp.einsum("uhp,shp->hus", cotan_blk, inputs_blk, preferred_element_type=jnp.float32)
    weights = decays * scores[None]
    joint = decays * pairs
    cotan_wide = cotan_blk.astype(jnp.float32)
    inputs_wide = inputs_blk.astype(jnp.float32)
    in_wide = in_blk.astype(jnp.float32)
    out_wide = out_blk.astype(jnp.float32)
    grad_inner = jnp.einsum("hus,uhp->shp", weights, cotan_wide, precision=highest)
    in_inner = jnp.einsum("hus,un->sn", joint, out_wide, precision=highest)
    out_inner = jnp.einsum("hts,sn->tn", joint, in_wide, precision=highest)
    product = joint * scores[None]
    column_totals = jnp.sum(product, axis=1)
    row_totals = jnp.sum(product, axis=2)
    inner = (
        jnp.dot(column_totals, upper, precision=highest)
        - jnp.dot(row_totals, upper, precision=highest)
        + row_totals
    )
    to_end = jnp.exp(running[:, -1:] - running)
    from_start = jnp.exp(running)
    state_part = jnp.einsum(
        "shp,sn->hpn", inputs_wide * to_end.T[:, :, None], in_wide, precision=highest
    )
    adjoint_part = jnp.einsum(
        "uhp,un->hpn", cotan_wide * from_start.T[:, :, None], out_wide, precision=highest
    )
    return (
        grad_inner,
        in_inner,
        out_inner,
        inner,
        running,
        state_part,
        adjoint_part,
        from_start[:, -1],
    )


def carried_block(pieces):
    inputs_blk, in_blk, out_blk, cotan_blk, running, grad_inner, inner, start_state, end_adjoint = (
        pieces
    )
    upper, lower = triangles(running.shape[1])
    to_end = jnp.exp(running[:, -1:] - running)
    from_start = jnp.exp(running)
    cotan_wide = cotan_blk.astype(jnp.float32)
    inputs_wide = inputs_blk.astype(jnp.float32)
    in_wide = in_blk.astype(jnp.float32)
    out_wide = out_blk.astype(jnp.float32)
    grad_block = (
        grad_inner
        + jnp.einsum("tn,hpn->thp", in_wide, end_adjoint, precision=highest) * to_end.T[:, :, None]
    )
    feed_out = jnp.einsum("thp,hpn->thn", cotan_wide, start_state, precision=highest)
    out_carried = jnp.einsum("ht,thn->tn", from_start, feed_out, precision=highest)
    from_state = from_start * jnp.einsum("thn,tn->ht", feed_out, out_wide, precision=highest)
    feed_in = jnp.einsum("thp,hpn->thn", inputs_wide, end_adjoint, precision=highest)
    in_carried = jnp.einsum("ht,thn->tn", to_end, feed_in, precision=highest)
    from_adjoint = to_end * jnp.einsum("thn,tn->ht", feed_in, in_wide, precision=highest)
    crossing = from_start[:, -1] * jnp.sum(end_adjoint * start_state, axis=(1, 2))
    own_term = jnp.einsum("thp,thp->ht", inputs_wide, grad_block, precision=highest)
    grad_rates = (
        inner
        + jnp.dot(from_state, lower, precision=highest)
        + jnp.dot(from_adjoint, upper, precision=highest)
        + crossing[:, None]
        - own_term
    )
    return (grad_block, in_carried, out_carried, grad_rates)


def combine(earlier, later):
    first_total, first_value = earlier
    second_total, second_value = later
    return (first_total * second_total, second_total[:, None, None] * first_value + second_value)


def carry_step(carry, item):
    value, factor = carry
    part, decay_total = item
    return ((decay_total[:, None, None] * value + part, factor * decay_total), (value, factor))


def on_device(inputs, in_map, out_map, log_decay, cotangent):
    heads_here = log_decay.shape[0]
    row_count = inputs.shape[0]
    head_width = inputs.shape[1] // heads_here
    blocks_here = row_count // BLOCK
    inputs_blocks = inputs.reshape(blocks_here, BLOCK, heads_here, head_width)
    cotan_blocks = cotangent.reshape(blocks_here, BLOCK, heads_here, head_width)
    in_blocks = in_map.reshape(blocks_here, BLOCK, in_map.shape[1])
    out_blocks = out_map.reshape(blocks_here, BLOCK, out_map.shape[1])
    rate_blocks = log_decay.reshape(heads_here, blocks_here, BLOCK).transpose(1, 0, 2)
    grad_inner, in_inner, out_inner, inner, running, state_parts, adjoint_parts, totals = lax.map(
        local_block, (inputs_blocks, in_blocks, out_blocks, rate_blocks, cotan_blocks)
    )
    zeros_state = jnp.zeros(state_parts.shape[1:], jnp.float32)
    ones_heads = jnp.ones((heads_here,), jnp.float32)
    (device_state, device_total), (start_states, before) = lax.scan(
        carry_step, (zeros_state, ones_heads), (state_parts, totals)
    )
    (device_adjoint, unused_total), (end_adjoints, after) = lax.scan(
        carry_step, (zeros_state, ones_heads), (adjoint_parts, totals), reverse=True
    )
    forward_pair = prefix(
        (device_total, device_state), "seq", combine, (ones_heads, zeros_state), False
    )
    backward_pair = prefix(
        (device_total, device_adjoint), "seq", combine, (ones_heads, zeros_state), True
    )
    state_in = forward_pair[1]
    adjoint_in = backward_pair[1]
    start_states = start_states + before[:, :, None, None] * state_in[None]
    end_adjoints = end_adjoints + after[:, :, None, None] * adjoint_in[None]
    grad_block, in_carried, out_carried, grad_rates = lax.map(
        carried_block,
        (
            inputs_blocks,
            in_blocks,
            out_blocks,
            cotan_blocks,
            running,
            grad_inner,
            inner,
            start_states,
            end_adjoints,
        ),
    )
    grad_inputs = grad_block.reshape(row_count, heads_here * head_width)
    grad_decay = grad_rates.transpose(1, 0, 2).reshape(heads_here, row_count)
    grad_in_map, grad_out_map = (
        lax.psum_scatter(
            (in_inner + in_carried).reshape(row_count, -1), "head", scatter_dimension=0, tiled=True
        ),
        lax.psum_scatter(
            (out_inner + out_carried).reshape(row_count, -1),
            "head",
            scatter_dimension=0,
            tiled=True,
        ),
    )
    return (grad_inputs, grad_in_map, grad_out_map, grad_decay)


def solution(mesh):
    placed = (P("seq", "head"), P("seq", None), P("seq", None), P("head", "seq"), P("seq", "head"))
    return jax.shard_map(
        on_device,
        mesh=mesh,
        in_specs=placed,
        out_specs=(
            P("seq", "head"),
            P(("seq", "head"), None),
            P(("seq", "head"), None),
            P("head", "seq"),
        ),
        check_vma=False,
    )
```

profile of v0, /device:TPU:1, one launch (start us, length us, event | category | flops | bytes accessed | tf_op | source)
XLA Modules:
  0.0 502.6 jit_solution(10394862926789882991)
XLA Ops:
  7.3 1.4 reshape.70
  8.7 2.2 reshape.74
  14.3 34.3 %while.108 = (s32[]{:T(128)}, f32[2,512,4,128]{1,3,2,0:T(8,128)}, f32[2,512,128]{2,1,0:T(8,128)}, f32[2,512,128]{2,1,0:T(8,128)}, f32[2,4,512]{2,1,0:T(4,128)S(1...) while((s32[]{:T(128)}, f32[2,512,4,128]{1,3,2,0:T(8,128)}, ...), condition=%wide.region_4.5_spmd, body=%wide.region_0.4_spmd.sunk | while | flops 3609462784 | bytes 46307800 | solution.py:137
  14.3 1.3 fusion.165
  15.6 1.4 constant_dynamic-slice_fusion.13
  17.8 3.7 multiply_reduce_fusion.3
  23.8 3.0 fusion.166
  28.5 1.4 fusion.172
  29.9 1.3 fusion.173
  31.5 1.3 fusion.165
  32.8 1.4 constant_dynamic-slice_fusion.13
  35.0 3.7 multiply_reduce_fusion.3
  41.0 3.0 fusion.166
  45.7 1.4 fusion.172
  47.1 1.4 fusion.173
  48.7 2.3 while.110
  48.8 1.1 bitcast_add_fusion.6
  52.7 1.8 while.111
  55.3 1.3 dynamic-slice
  57.5 68.1 %all-reduce = f32[128]{0:T(128)S(1)} all-reduce(f32[128]{0:T(128)S(1)} %dynamic-update-slice), channel_id=2, replica_groups=mesh['seq'=32,'head'=16] {'seq'}, use_global_device_ids=true, to_apply=%add | all-reduce | flops 128 | bytes 1024
  125.8 35.8 %all-gather.6.cloned.1.call-done = f32[128,128,128]{2,1,0:T(8,128)} async-done(((f32[4,128,128]{2,1,0:T(8,128)}), f32[128,128,128]{2,1,0:T(8,128)}) %all-gather.6.cloned.1.call-update) | async-done | bytes 8388624 | tf_op jit(solution)/shard_map/all_gather | solution.py:14
  161.5 35.4 %while.112 = (s32[]{:T(128)}, f32[4,128,128]{2,1,0:T(8,128)S(1)}, s32[]{:T(128)}, f32[32,4]{1,0:T(8,128)S(1)}, f32[32,4,128,128]{3,2,1,0:T(8,128)}, /*index=5*/s32[]{:T(128)}, s32[]{:T(128)}, s32[]{:T(128)}, s32[]{:T(128)}) while((s32[]{:T(128)}, f32[4,128,128]{2,1,0:T(8,128)S(1)}, s32[]{:T(128)}, f32[32,4]{1,0:T(8,128)S(1)}, ...), condition=%wide.region_12.13_spmd.clone, body=%wide.region_11.12_spmd.clone.sunk | while | flops 262152 | bytes 786647 | solution.py:27
  175.9 1.1 fusion.197
  197.0 68.7 %all-gather.8.cloned.1.call-done = f32[128,128,128]{2,1,0:T(8,128)} async-done(((f32[4,128,128]{2,1,0:T(8,128)}), f32[128,128,128]{2,1,0:T(8,128)}) %all-gather.8.cloned.1.call-update) | async-done | bytes 8388624 | tf_op jit(solution)/shard_map/all_gather | solution.py:14
  265.7 35.0 %while.113 = (s32[]{:T(128)}, f32[4,128,128]{2,1,0:T(8,128)S(1)}, s32[]{:T(128)}, f32[32,4]{1,0:T(8,128)S(1)}, f32[32,4,128,128]{3,2,1,0:T(8,128)}, /*index=5*/s32[]{:T(128)}, s32[]{:T(128)}) while((s32[]{:T(128)}, f32[4,128,128]{2,1,0:T(8,128)S(1)}, s32[]{:T(128)}, f32[32,4]{1,0:T(8,128)S(1)}, f32[32,4,128,128]{3,2,1,0:T(8,128)}, ...), condition=%wide.region_8.9_spmd.clone, body=%wide.region_7.8_spmd.clone.sunk | while | flops 262148 | bytes 786585 | solution.py:27
  300.7 1.1 multiply_add_fusion
  304.1 74.5 %while.109 = (s32[]{:T(128)}, f32[2,512,4,128]{3,2,1,0:T(4,128)}, f32[2,512,128]{2,1,0:T(8,128)}, f32[2,512,128]{2,1,0:T(8,128)}, f32[2,4,512]{2,1,0:T(4,128)}, ...) while((s32[]{:T(128)}, f32[2,512,4,128]{3,2,1,0:T(4,128)}, ...), condition=%wide.region_15.16_spmd, body=%wide.region_13.15_spmd.sunk | while | flops 1247686656 | bytes 51973800 | solution.py:158
  305.3 1.2 constant_dynamic-slice_fusion.14
  306.6 1.3 constant_dynamic-slice_fusion.16
  308.2 2.0 fusion.187
  310.2 1.2 constant_dynamic-slice_fusion.17
  312.1 1.3 copy.123
  314.3 3.0 fusion.190
  317.3 1.3 convolution_add_fusion.3
  318.5 1.2 fusion.192
  319.7 1.2 fusion.193
  320.9 1.6 convolution_bitcast_fusion.9
  322.5 1.3 copy.124
  323.8 3.2 fusion.191
  327.0 1.7 fusion.194
  328.8 4.7 fusion.189
  333.5 4.5 fusion.188
  339.6 1.7 copy_dynamic-update-slice_fusion.2
  342.6 1.2 constant_dynamic-slice_fusion.14
  343.8 1.3 constant_dynamic-slice_fusion.16
  345.5 2.0 fusion.187
  347.5 1.2 constant_dynamic-slice_fusion.17
  349.3 1.3 copy.123
  351.5 3.0 fusion.190
  354.6 1.3 convolution_add_fusion.3
  355.8 1.2 fusion.192
  357.0 1.2 fusion.193
  358.2 1.6 convolution_bitcast_fusion.9
  359.8 1.3 copy.124
  361.1 3.2 fusion.191
  364.3 1.7 fusion.194
  366.0 4.7 fusion.189
  370.7 4.5 fusion.188
  376.9 1.6 copy_dynamic-update-slice_fusion.2
  378.5 2.1 add.148
  380.7 2.0 add.147
  382.7 3.1 copy.96
  385.8 48.9 %reduce-scatter.5.cloned.1.call-done = f32[64,128]{1,0:T(8,128)} async-done(((f32[1024,128]{1,0:T(8,128)}), f32[64,128]{1,0:T(8,128)}) %reduce-scatter.5.cloned.1.call-update) | async-done | bytes 32784 | tf_op jit(solution)/shard_map/reduce_scatter | solution.py:178
  434.7 61.3 %reduce-scatter.3.cloned.1.call-done = f32[64,128]{1,0:T(8,128)} async-done(((f32[1024,128]{1,0:T(8,128)}), f32[64,128]{1,0:T(8,128)}) %reduce-scatter.3.cloned.1.call-update) | async-done | bytes 32784 | tf_op jit(solution)/shard_map/reduce_scatter | solution.py:175
  (315 shorter events, 97.7 us)
Async XLA Ops:
  7.2 7.1 %copy-start.5 = (bf16[1024,128]{1,0:T(8,128)(2,1)S(1)}, bf16[1024,128]{1,0:T(8,128)(2,1)}, u32[]{:S(2)}) copy-start(bf16[1024,128]{1,0:T(8,128)(2,1)} %param.19) | copy-start | bytes 786436
  7.2 7.1 %copy-start = (bf16[1024,128]{1,0:T(8,128)(2,1)S(1)}, bf16[1024,128]{1,0:T(8,128)(2,1)}, u32[]{:S(2)}) copy-start(bf16[1024,128]{1,0:T(8,128)(2,1)} %param.18) | copy-start | bytes 786436
  7.2 7.1 %copy-start.27 = (f32[4,1024]{1,0:T(4,128)S(1)}, f32[4,1024]{1,0:T(4,128)}, u32[]{:S(2)}) copy-start(f32[4,1024]{1,0:T(4,128)} %param.20) | copy-start | bytes 49156
  7.2 154.3 %all-gather.6.cloned.1.call-start = ((), (), s32[]{:S(2)}) async-start(), calls=%async_computation.4 | async-start | bytes 8650752 | tf_op jit(solution)/shard_map/all_gather | solution.py:14
  17.8 4.4 copy-start.14
  17.8 5.4 %copy-start.16 = (f32[2,512,128]{2,1,0:T(8,128)S(1)}, f32[2,512,128]{2,1,0:T(8,128)}, u32[]{:S(2)}) copy-start(f32[2,512,128]{2,1,0:T(8,128)} %get-tuple-element.1271) | copy-start | bytes 1572868 | tf_op jit(solution)/shard_map/while
  17.8 6.0 %copy-start.9 = (f32[512,512]{1,0:T(8,128)S(1)}, f32[512,512]{1,0:T(8,128)}, u32[]{:S(2)}) copy-start(f32[512,512]{1,0:T(8,128)} %fusion.165) | copy-start | bytes 3145732 | tf_op jit(solution)/shard_map/while
  17.8 6.0 %copy-start.11 = (f32[2,512,4,128]{1,3,2,0:T(8,128)S(1)}, f32[2,512,4,128]{1,3,2,0:T(8,128)}, u32[]{:S(2)}) copy-start(f32[2,512,4,128]{1,3,2,0:T(8,128)} %get-tuple-element.1269) | copy-start | bytes 6291460 | tf_op jit(solution)/shard_map/while
  23.2 3.7 copy-start.15
  23.8 3.1 copy-start.17
  26.9 1.3 copy-start.12
  34.9 4.3 copy-start.14
  34.9 5.4 %copy-start.16 = (f32[2,512,128]{2,1,0:T(8,128)S(1)}, f32[2,512,128]{2,1,0:T(8,128)}, u32[]{:S(2)}) copy-start(f32[2,512,128]{2,1,0:T(8,128)} %get-tuple-element.1271) | copy-start | bytes 1572868 | tf_op jit(solution)/shard_map/while
  35.0 6.0 %copy-start.9 = (f32[512,512]{1,0:T(8,128)S(1)}, f32[512,512]{1,0:T(8,128)}, u32[]{:S(2)}) copy-start(f32[512,512]{1,0:T(8,128)} %fusion.165) | copy-start | bytes 3145732 | tf_op jit(solution)/shard_map/while
  35.0 6.0 %copy-start.11 = (f32[2,512,4,128]{1,3,2,0:T(8,128)S(1)}, f32[2,512,4,128]{1,3,2,0:T(8,128)}, u32[]{:S(2)}) copy-start(f32[2,512,4,128]{1,3,2,0:T(8,128)} %get-tuple-element.1269) | copy-start | bytes 6291460 | tf_op jit(solution)/shard_map/while
  40.3 3.7 copy-start.15
  41.0 3.1 copy-start.17
  44.0 1.3 copy-start.12
  48.6 4.0 copy-start.13
  51.1 0.7 copy-start.3
  51.8 213.9 %all-gather.8.cloned.1.call-start = ((), (), s32[]{:S(2)}) async-start(), calls=%async_computation.5 | async-start | bytes 8650752 | tf_op jit(solution)/shard_map/all_gather | solution.py:14
  54.5 0.7 copy-start.4
  55.2 245.5 %copy-start.22 = (f32[2,4,128,128]{3,2,1,0:T(8,128)S(1)}, f32[2,4,128,128]{3,2,1,0:T(8,128)}, u32[]{:S(2)}) copy-start(f32[2,4,128,128]{3,2,1,0:T(8,128)} %get-tuple-element.577) | copy-start | bytes 1572868
  55.2 379.5 %reduce-scatter.5.cloned.1.call-start = ((), (), s32[]{:S(2)}) async-start(), calls=%async_computation.3 | async-start | bytes 557056 | tf_op jit(solution)/shard_map/reduce_scatter | solution.py:178
  304.1 1.3 copy-start.1
  304.1 2.5 copy-start.6
  304.1 6.1 %copy-start.23 = (f32[2,4,512]{2,1,0:T(4,128)}, f32[2,4,512]{2,1,0:T(4,128)S(1)}, u32[]{:S(2)}) copy-start(f32[2,4,512]{2,1,0:T(4,128)S(1)} %get-tuple-element.1444) | copy-start | bytes 49156 | tf_op jit(solution)/shard_map/while
  304.1 6.1 %copy-start.25 = (f32[2,4,512]{2,1,0:T(4,128)}, f32[2,4,512]{2,1,0:T(4,128)S(1)}, u32[]{:S(2)}) copy-start(f32[2,4,512]{2,1,0:T(4,128)S(1)} %get-tuple-element.1440) | copy-start | bytes 49156 | tf_op jit(solution)/shard_map/while
  308.2 3.2 copy-start.10
  323.8 9.6 %copy-start.8 = (f32[512,4,128]{2,1,0:T(4,128)S(1)}, f32[512,4,128]{2,1,0:T(4,128)}, u32[]{:S(2)}) copy-start(f32[512,4,128]{2,1,0:T(4,128)} %copy.123) | copy-start | bytes 3145732 | tf_op jit(solution)/shard_map/while
  323.8 14.1 %copy-start.18 = (f32[2,512,128]{2,1,0:T(8,128)S(1)}, f32[2,512,128]{2,1,0:T(8,128)}, u32[]{:S(2)}) copy-start(f32[2,512,128]{2,1,0:T(8,128)} %get-tuple-element.1419) | copy-start | bytes 1572868 | tf_op jit(solution)/shard_map/while
  323.8 14.1 %copy-start.20 = (f32[2,512,128]{2,1,0:T(8,128)S(1)}, f32[2,512,128]{2,1,0:T(8,128)}, u32[]{:S(2)}) copy-start(f32[2,512,128]{2,1,0:T(8,128)} %get-tuple-element.1420) | copy-start | bytes 1572868 | tf_op jit(solution)/shard_map/while
  327.0 14.3 %copy-start.2 = (bf16[2,512,4,128]{3,2,1,0:T(4,128)(2,1)S(1)}, bf16[2,512,4,128]{3,2,1,0:T(4,128)(2,1)}, u32[]{:S(2)}) copy-start(bf16[2,512,4,128]{3,2,1,0:T(4,128)(2,1)} %copy-done.1) | copy-start | bytes 3145732 | tf_op jit(solution)/shard_map/while
  327.0 14.3 %copy-start.7 = (bf16[2,512,128]{2,1,0:T(8,128)(2,1)S(1)}, bf16[2,512,128]{2,1,0:T(8,128)(2,1)}, u32[]{:S(2)}) copy-start(bf16[2,512,128]{2,1,0:T(8,128)(2,1)} %copy-done.6) | copy-start | bytes 786436 | tf_op jit(solution)/shard_map/while
  327.0 14.3 %copy-start.24 = (f32[2,4,512]{2,1,0:T(4,128)S(1)}, f32[2,4,512]{2,1,0:T(4,128)}, u32[]{:S(2)}) copy-start(f32[2,4,512]{2,1,0:T(4,128)} %copy-done.23) | copy-start | bytes 49156 | tf_op jit(solution)/shard_map/while
  327.0 14.3 %copy-start.26 = (f32[2,4,512]{2,1,0:T(4,128)S(1)}, f32[2,4,512]{2,1,0:T(4,128)}, u32[]{:S(2)}) copy-start(f32[2,4,512]{2,1,0:T(4,128)} %copy-done.25) | copy-start | bytes 49156 | tf_op jit(solution)/shard_map/while
  338.0 0.8 copy-start.19
  338.8 0.8 copy-start.21
  341.3 1.3 copy-start.1
  341.3 2.5 copy-start.6
  341.3 6.1 %copy-start.23 = (f32[2,4,512]{2,1,0:T(4,128)}, f32[2,4,512]{2,1,0:T(4,128)S(1)}, u32[]{:S(2)}) copy-start(f32[2,4,512]{2,1,0:T(4,128)S(1)} %get-tuple-element.1444) | copy-start | bytes 49156 | tf_op jit(solution)/shard_map/while
  341.4 6.1 %copy-start.25 = (f32[2,4,512]{2,1,0:T(4,128)}, f32[2,4,512]{2,1,0:T(4,128)S(1)}, u32[]{:S(2)}) copy-start(f32[2,4,512]{2,1,0:T(4,128)S(1)} %get-tuple-element.1440) | copy-start | bytes 49156 | tf_op jit(solution)/shard_map/while
  345.5 3.2 copy-start.10
  361.1 9.6 %copy-start.8 = (f32[512,4,128]{2,1,0:T(4,128)S(1)}, f32[512,4,128]{2,1,0:T(4,128)}, u32[]{:S(2)}) copy-start(f32[512,4,128]{2,1,0:T(4,128)} %copy.123) | copy-start | bytes 3145732 | tf_op jit(solution)/shard_map/while
  361.1 14.1 %copy-start.18 = (f32[2,512,128]{2,1,0:T(8,128)S(1)}, f32[2,512,128]{2,1,0:T(8,128)}, u32[]{:S(2)}) copy-start(f32[2,512,128]{2,1,0:T(8,128)} %get-tuple-element.1419) | copy-start | bytes 1572868 | tf_op jit(solution)/shard_map/while
  361.1 14.1 %copy-start.20 = (f32[2,512,128]{2,1,0:T(8,128)S(1)}, f32[2,512,128]{2,1,0:T(8,128)}, u32[]{:S(2)}) copy-start(f32[2,512,128]{2,1,0:T(8,128)} %get-tuple-element.1420) | copy-start | bytes 1572868 | tf_op jit(solution)/shard_map/while
  364.3 14.2 %copy-start.2 = (bf16[2,512,4,128]{3,2,1,0:T(4,128)(2,1)S(1)}, bf16[2,512,4,128]{3,2,1,0:T(4,128)(2,1)}, u32[]{:S(2)}) copy-start(bf16[2,512,4,128]{3,2,1,0:T(4,128)(2,1)} %copy-done.1) | copy-start | bytes 3145732 | tf_op jit(solution)/shard_map/while
  364.3 14.2 %copy-start.7 = (bf16[2,512,128]{2,1,0:T(8,128)(2,1)S(1)}, bf16[2,512,128]{2,1,0:T(8,128)(2,1)}, u32[]{:S(2)}) copy-start(bf16[2,512,128]{2,1,0:T(8,128)(2,1)} %copy-done.6) | copy-start | bytes 786436 | tf_op jit(solution)/shard_map/while
  364.3 14.2 %copy-start.24 = (f32[2,4,512]{2,1,0:T(4,128)S(1)}, f32[2,4,512]{2,1,0:T(4,128)}, u32[]{:S(2)}) copy-start(f32[2,4,512]{2,1,0:T(4,128)} %copy-done.23) | copy-start | bytes 49156 | tf_op jit(solution)/shard_map/while
  364.3 14.2 %copy-start.26 = (f32[2,4,512]{2,1,0:T(4,128)S(1)}, f32[2,4,512]{2,1,0:T(4,128)}, u32[]{:S(2)}) copy-start(f32[2,4,512]{2,1,0:T(4,128)} %copy-done.25) | copy-start | bytes 49156 | tf_op jit(solution)/shard_map/while
  375.3 0.8 copy-start.19
  376.1 0.8 copy-start.21
  380.6 115.4 %reduce-scatter.3.cloned.1.call-start = ((), (), s32[]{:S(2)}) async-start(), calls=%async_computation.2 | async-start | bytes 557056 | tf_op jit(solution)/shard_map/reduce_scatter | solution.py:175
Sparse Core Ops, SparseCore 0:
  51.9 109.5 all-gather.5
  164.7 100.9 all-gather.7
  380.7 53.9 reduce-scatter.4
  438.1 57.8 reduce-scatter.2
where the time goes:
time: 507 us; the launch traced here: 503 us
  waiting for transfers between devices  215 us (42%)
  other arithmetic  83.6 us (16%)
  matrix products  71.4 us (14%)
  blocking collectives  68.1 us (13%)
  local copies, waits for them, and re-layouts  46.6 us (9%)
  between operations  14.7 us (3%)
    all_gather x2, waiting for transfers between devices, prefix(): everything = jax.tree.map(lambda part: lax.all_gather(part, axis), array)  104 us
    unnamed x1, blocking collectives  68.1 us
    select_n x64, other arithmetic, hop(): return jax.tree.map(lambda a, b: jnp.where(reached, a, b), new, before)  67.5 us
    reduce_scatter x1, waiting for transfers between devices, on_device(): lax.psum_scatter((in_inner + in_carried).reshape(row_count, -1), 'head',...  61.3 us
    reduce_scatter x1, waiting for transfers between devices, on_device(): lax.psum_scatter((out_inner + out_carried).reshape(row_count, -1), 'head'...  48.9 us
  transfers between devices with their start and end apart: 4, of which 4 were waited for; matrix products, arithmetic and copies ran while one was open for 9% of the time, Pallas kernels for 0%

commit v1 on v0

v1 whole, which is shorter than its diff:
```python
import jax
import jax.numpy as jnp
from jax import lax
from jax.experimental import pallas as pl
from jax.experimental.pallas import tpu as pltpu
from jax.sharding import Mesh, PartitionSpec as P

f32, bf16 = jnp.float32, jnp.bfloat16
SEQ, HEAD = ("x", "z"), ("y", "core")
TOK, HEADS, DIM, TILE = 1024, 4, 128, 128
BLOCKS = TOK // TILE
VMEM = 56 << 20


def dot(a, b, dims):
    return lax.dot_general(a, b, (dims, ((), ())), preferred_element_type=f32)


def split(v):
    hi = v.astype(bf16)
    return hi, (v - hi.astype(f32)).astype(bf16)


def dot_wide(wide, exact):
    return dot(jnp.concatenate(split(wide), axis=1), jnp.concatenate([exact, exact], axis=0), ((1,), (0,)))


def running_sums(v, width, shift_suffix=True):
    lanes = v.shape[1]
    at = lax.broadcasted_iota(jnp.int32, v.shape, 1) & (width - 1)
    prefix = v
    suffix = jnp.where(at < width - 1, pltpu.roll(v, lanes - 1, 1), 0.0) if shift_suffix else v
    step = 1
    while step < width:
        prefix = prefix + jnp.where(at >= step, pltpu.roll(prefix, step, 1), 0.0)
        suffix = suffix + jnp.where(at < width - step, pltpu.roll(suffix, lanes - step, 1), 0.0)
        step *= 2
    return prefix, suffix


def state_kernel(x_ref, dy_ref, b_ref, c_ref, rate_ref, piece_ref, rows_ref):
    rates = jnp.concatenate([rate_ref[...], rate_ref[...]], axis=0)
    prefix, suffix = running_sums(rates, TOK)
    row = lax.broadcasted_iota(jnp.int32, rates.shape, 0)
    rows = jnp.exp(jnp.where(row < HEADS, suffix, prefix))
    rows_ref[...] = rows
    totals = jnp.broadcast_to(jnp.exp(prefix[:, TOK - 1 :]), (8, DIM))
    pair = (totals, jnp.concatenate([totals[2:], totals[:2]], axis=0))
    for k in range(32):
        piece_ref[k, 32:40, :] = pair[k % 2]
    maps = (b_ref[...].astype(f32).T, c_ref[...].astype(f32).T)
    for h in range(HEADS):
        for d, ref in enumerate((x_ref, dy_ref)):
            scaled = maps[d] * rows[d * HEADS + h : d * HEADS + h + 1]
            both = dot(jnp.concatenate(split(scaled), axis=0), ref[:, h * DIM : (h + 1) * DIM], ((1,), (0,)))
            state = both[:DIM] + both[DIM:]
            at = (d * 2 + h % 2) * 8
            for k in range(16):
                piece_ref[2 * k + h // 2, at : at + 8, :] = state[8 * k : 8 * k + 8]


def scan_kernel(got_ref, out_ref):
    for half in range(2):
        at = half * 8
        held = jnp.zeros((8, DIM), f32)
        for k in range(32):
            out_ref[k, at : at + 8, :] = held
            held = held * got_ref[k, 32 + half : 33 + half, :] + got_ref[k, at : at + 8, :]
        at = 16 + half * 8
        held = jnp.zeros((8, DIM), f32)
        for k in reversed(range(32)):
            out_ref[k, at : at + 8, :] = held
            held = held * got_ref[k, 32 + half : 33 + half, :] + got_ref[k, at : at + 8, :]


def piece_of(got_ref, d, h):
    at = (d * 2 + h % 2) * 8
    return jnp.concatenate([got_ref[2 * k + h // 2, at : at + 8, :] for k in range(16)], axis=0)


def local_kernel(first, x_ref, dy_ref, b_ref, c_ref, rate_ref, *refs):
    if first == 0:
        rows_ref, gx_ref, maps_ref, decay_ref, cols_ref, rb, sb, tb, rs, acc, ec = refs
        maps_ref[...] = jnp.zeros(maps_ref.shape, f32)
    else:
        before_ref, gx_ref, maps_ref, decay_ref, rb, sb, tb, rs, acc, ec = refs
        maps_ref[...] = before_ref[...]
    rates = jnp.concatenate([rate_ref[...], rate_ref[...]], axis=0)
    prefix, suffix = running_sums(rates, TILE)
    for k in range(BLOCKS):
        rb[k] = prefix[:, k * TILE : (k + 1) * TILE]
        sb[k] = suffix[:, k * TILE : (k + 1) * TILE]
        tb[k] = jnp.broadcast_to(prefix[:, (k + 1) * TILE - 1 : (k + 1) * TILE], (8, TILE))
        if first == 0:
            rows = rows_ref[:, k * TILE : (k + 1) * TILE]
            cols_ref[k * TILE : (k + 1) * TILE, :] = jnp.concatenate([rows] * 16, axis=0).T
    rs[...] = jnp.zeros(rs.shape, f32)
    causal = lax.broadcasted_iota(jnp.int32, (TILE, TILE), 0) <= lax.broadcasted_iota(jnp.int32, (TILE, TILE), 1)

    def pair(j, i, decays, new):
        sj = pl.ds(pl.multiple_of(j * TILE, TILE), TILE)
        si = pl.ds(pl.multiple_of(i * TILE, TILE), TILE)
        b, c = b_ref[sj, :], c_ref[si, :]
        scores = dot(b, c, ((1,), (1,)))
        joint = None
        for k in range(2):
            lanes = slice(k * DIM, (k + 1) * DIM)
            dy = dy_ref[si, lanes]
            decay = decays(k)
            pairs = dot(x_ref[sj, lanes], dy, ((1,), (1,)))
            weights = decay * scores
            mine = decay * pairs
            joint = mine if joint is None else joint + mine
            product = weights * pairs
            gx = dot_wide(weights, dy)
            if new:
                gx_ref[sj, lanes] = gx
                acc[k] = product
            else:
                gx_ref[sj, lanes] += gx
                acc[k] += product
            rs[i, k : k + 1, :] += jnp.sum(product, axis=0, keepdims=True)
        maps_ref[sj, :DIM] += dot_wide(joint, c)
        maps_ref[si, DIM:] += dot_wide(joint.T, b)

    def outer(j, nothing):
        own, rest = rb[j], sb[j]

        def inside(k):
            across = jnp.broadcast_to(own[first + k : first + k + 1], (TILE, TILE))
            return jnp.where(causal, jnp.exp(across - across.T), 0.0)

        pair(j, j, inside, True)
        for k in range(2):
            ec[k] = jnp.broadcast_to(jnp.exp(rest[first + k : first + k + 1]), (TILE, TILE)).T

        def inner(i, between):
            from_start = jnp.exp(rb[i] + between)
            pair(j, i, lambda k: ec[k] * from_start[first + k : first + k + 1], False)
            return between + tb[i]

        lax.fori_loop(j + 1, BLOCKS, inner, jnp.zeros((8, TILE), f32))
        for k in range(2):
            decay_ref[j, k : k + 1, :] = jnp.sum(acc[k].T, axis=0, keepdims=True)
        return nothing

    lax.fori_loop(0, BLOCKS, outer, 0)
    for k in range(BLOCKS):
        decay_ref[k, 0:2, :] = decay_ref[k, 0:2, :] - rs[k, 0:2, :]


def twice(v):
    return jnp.concatenate([v, v], axis=1)


def maps_kernel(core_ref, got_ref, x_ref, dy_ref, cols_ref, local_ref, keep_ref, send_ref, parts):
    @pl.when(pl.program_id(0) == 0)
    def _():
        for d in range(2):
            for h in range(HEADS):
                parts[d * HEADS + h] = jnp.concatenate(split(piece_of(got_ref, d, h)), axis=1)

    grads = []
    for d, ref in ((1, x_ref), (0, dy_ref)):
        total = local_ref[:, (1 - d) * DIM : (2 - d) * DIM]
        for h in range(HEADS):
            at = (1 - d) * HEADS + h
            fed = dot(twice(ref[:, h * DIM : (h + 1) * DIM]), parts[d * HEADS + h], ((1,), (1,)))
            total = total + cols_ref[:, at : at + 1] * fed
        grads.append(total)
    for core in range(2):
        for there in (core, 1 - core):
            out = keep_ref if there == core else send_ref

            @pl.when(core_ref[0] == core)
            def _():
                for k in range(out.shape[0]):
                    at = (2 * k + there) * 64
                    out[k, :, :DIM] = grads[0][at : at + 64]
                    out[k, :, DIM:] = grads[1][at : at + 64]


def rest_kernel(got_ref, x_ref, dy_ref, b_ref, c_ref, cols_ref, rows_ref, gxa_ref, gxb_ref, da_ref, db_ref,
                gx_ref, decay_ref, parts, stacked, sums):
    step = pl.program_id(0)
    tile = x_ref.shape[0]

    @pl.when(step == 0)
    def _():
        for h in range(HEADS):
            for d in range(2):
                parts[d * HEADS + h] = jnp.concatenate(split(piece_of(got_ref, d, h)), axis=1)
            stacked[h] = jnp.concatenate(split(piece_of(got_ref, 1, h)), axis=0)

    b, c = b_ref[...], c_ref[...]
    wide_b, wide_c = b.astype(f32), c.astype(f32)
    for h in range(HEADS):
        lanes = slice(h * DIM, (h + 1) * DIM)
        local = (gxa_ref, gxb_ref)[h // 2][:, (h % 2) * DIM : (h % 2 + 1) * DIM]
        gx_ref[:, lanes] = local + cols_ref[:, h : h + 1] * dot(twice(b), stacked[h], ((1,), (0,)))
        fed = dot(twice(x_ref[:, lanes]), parts[HEADS + h], ((1,), (1,))) * wide_b
        sums[step, h : h + 1, :] = jnp.sum(fed.T, axis=0, keepdims=True)
        fed = dot(twice(dy_ref[:, lanes]), parts[h], ((1,), (1,))) * wide_c
        sums[step, HEADS + h : HEADS + h + 1, :] = jnp.sum(fed.T, axis=0, keepdims=True)

    @pl.when(step == TOK // tile - 1)
    def _():
        rows = rows_ref[...]
        terms = jnp.concatenate([sums[k] for k in range(TOK // tile)], axis=1) * rows
        local = [jnp.concatenate([ref[k, 0:2, :] for k in range(BLOCKS)], axis=1) for ref in (da_ref, db_ref)]
        terms = terms + jnp.concatenate(local + [jnp.zeros((HEADS, TOK), f32)], axis=0)
        at = lax.broadcasted_iota(jnp.int32, terms.shape, 1)
        moved = jnp.where(at >= 1, pltpu.roll(terms, 1, 1), 0.0)
        prefix, _ = running_sums(moved, TOK, False)
        _, suffix = running_sums(terms, TOK, False)
        decay = prefix[:HEADS] + suffix[HEADS:]
        which = lax.broadcasted_iota(jnp.int32, (HEADS, 1), 0)
        crossing = jnp.zeros((HEADS, 1), f32)
        for h in range(HEADS):
            both = jnp.sum(piece_of(got_ref, 0, h) * piece_of(got_ref, 1, h), axis=0, keepdims=True)
            both = jnp.sum(both, axis=1, keepdims=True)
            crossing = jnp.where(which == h, both, crossing)
        decay_ref[...] = decay + crossing * rows[HEADS:, TOK - 1 :]


def params():
    return pltpu.CompilerParams(vmem_limit_bytes=VMEM)


def shape(*dims, dtype=f32):
    return jax.ShapeDtypeStruct(dims, dtype)


def whole(*dims):
    return pl.BlockSpec(dims, lambda *_: (0,) * len(dims))


def local_pairs(first, x, dy, b, c, rates, other):
    half = pl.BlockSpec((TOK, 2 * DIM), lambda *_: (0, first // 2))
    outs = [shape(TOK, 2 * DIM), shape(TOK, 2 * DIM), shape(BLOCKS, 8, TILE)]
    if first == 0:
        outs.append(shape(TOK, DIM))
    return pl.pallas_call(
        lambda *refs: local_kernel(first, *refs),
        grid=(1,),
        in_specs=[half, half, whole(TOK, DIM), whole(TOK, DIM), whole(HEADS, TOK), whole(*other.shape)],
        out_specs=[whole(*o.shape) for o in outs],
        out_shape=outs,
        scratch_shapes=[pltpu.VMEM((BLOCKS, 8, TILE), f32)] * 4 + [pltpu.VMEM((2, TILE, TILE), f32)] * 2,
        compiler_params=params(),
        name=f"local_{first}",
    )(x, dy, b, c, rates, other)


def on_device(inputs, in_map, out_map, log_decay, cotangent):
    pieces, rows = pl.pallas_call(
        state_kernel,
        out_shape=[shape(32, 40, DIM), shape(8, TOK)],
        compiler_params=params(),
        name="states",
    )(inputs, cotangent, in_map, out_map, log_decay)
    got = lax.all_to_all(pieces, SEQ, 0, 0)
    gx_a, maps, decay_a, cols = local_pairs(0, inputs, cotangent, in_map, out_map, log_decay, rows)
    got, maps = lax.optimization_barrier((got, maps))
    scanned = pl.pallas_call(
        scan_kernel, out_shape=shape(32, 32, DIM), compiler_params=params(), name="scan"
    )(got)
    scanned, maps = lax.optimization_barrier((scanned, maps))
    got = lax.all_to_all(scanned, SEQ, 0, 0)
    gx_b, maps, decay_b = local_pairs(2, inputs, cotangent, in_map, out_map, log_decay, maps)
    got, maps = lax.optimization_barrier((got, maps))
    tile = 256
    steps = TOK // tile
    parts = pltpu.VMEM((2 * HEADS, DIM, 2 * DIM), bf16)
    heads = pl.BlockSpec((tile, HEADS * DIM), lambda i: (i, 0))
    pair = pl.BlockSpec((tile, 2 * DIM), lambda i: (i, 0))
    one = pl.BlockSpec((tile, DIM), lambda i: (i, 0))
    piece = whole(32, 32, DIM)
    core = lax.axis_index("core").astype(jnp.int32).reshape(1)
    rows_of = pl.BlockSpec((steps // 2, 64, 2 * DIM), lambda i: (i, 0, 0))
    keep, send = pl.pallas_call(
        maps_kernel,
        grid=(steps,),
        in_specs=[pl.BlockSpec(memory_space=pltpu.SMEM), piece, heads, heads, one, pair],
        out_specs=[rows_of, rows_of],
        out_shape=[shape(8, 64, 2 * DIM)] * 2,
        scratch_shapes=[parts],
        compiler_params=params(),
        name="maps",
    )(core, got, inputs, cotangent, cols, maps)
    reduced = keep + lax.ppermute(send, "core", [(0, 1), (1, 0)])
    reduced, got = lax.optimization_barrier((reduced, got))
    reduced = lax.all_to_all(reduced, "y", 0, 0)
    grad_inputs, grad_decay = pl.pallas_call(
        rest_kernel,
        grid=(steps,),
        in_specs=[
            piece, heads, heads, one, one, one, whole(8, TOK), pair, pair,
            whole(BLOCKS, 8, TILE), whole(BLOCKS, 8, TILE),
        ],
        out_specs=[heads, whole(HEADS, TOK)],
        out_shape=[shape(TOK, HEADS * DIM), shape(HEADS, TOK)],
        scratch_shapes=[parts, pltpu.VMEM((HEADS, 2 * DIM, DIM), bf16), pltpu.VMEM((steps, 8, tile), f32)],
        compiler_params=params(),
        name="rest",
    )(got, inputs, cotangent, in_map, out_map, cols, rows, gx_a, gx_b, decay_a, decay_b)
    reduced, grad_decay = lax.optimization_barrier((reduced, grad_decay))
    total = jnp.sum(reduced, axis=0)
    return (grad_inputs, total[:, :DIM], total[:, DIM:], grad_decay)


def solution(mesh):
    grid = Mesh(mesh.devices.reshape(4, 8, 8, 2), SEQ + HEAD)
    rows, columns = P(SEQ, None), P(SEQ, HEAD)
    return jax.shard_map(
        on_device,
        mesh=grid,
        in_specs=(columns, rows, rows, P(HEAD, SEQ), columns),
        out_specs=(columns, P(SEQ + HEAD, None), P(SEQ + HEAD, None), P(HEAD, SEQ)),
        check_vma=False,
    )
```

time: 507 us -> 120 us (0.24)
  waiting for transfers between devices: 215 us -> 12.8 us
  other arithmetic: 83.6 us -> 1.96 us
  matrix products: 71.4 us -> 0 us
  blocking collectives: 68.1 us -> 0 us
  Pallas kernels: 0 us -> 68 us
  local copies, waits for them, and re-layouts: 46.6 us -> 2.29 us
  starting transfers between devices: 0.16 us -> 33.2 us
  between operations: 14.7 us -> 0.67 us
    reduce_scatter x2 -> x0, waiting for transfers between devices: 110 us -> none  [the longest x1 61.3 us: on_device(): lax.psum_scatter((in_inner + in_carried).reshape(row_count, -1), 'head',...]
    all_gather x2 -> x0, waiting for transfers between devices: 104 us -> none  [prefix(): everything = jax.tree.map(lambda part: lax.all_gather(part, axis), array)]
    dot_general x38 -> x0, matrix products: 71.4 us -> none  [the longest x2 9.37 us: carried_block(): in_carried = jnp.einsum('ht,thn->tn', to_end, feed_in, precision=highest)]
    unnamed x1 -> x0, blocking collectives: 68.1 us -> none
    pallas_call x0 -> x6, Pallas kernels: none -> 68 us  [the longest x2 49.3 us: local_pairs(): pl.pallas_call(lambda *refs: local_kernel(first, *refs), grid=(1,), in_sp...]
    select_n x64 -> x0, other arithmetic: 67.5 us -> none  [hop(): return jax.tree.map(lambda a, b: jnp.where(reached, a, b), new, before)]
    all_to_all x0 -> x3, starting transfers between devices: none -> 29.8 us  [the longest x1 13.7 us: on_device(): got = lax.all_to_all(pieces, SEQ, 0, 0)]
    dynamic_slice x18 -> x0, local copies, waits for them, and re-layouts: 12.6 us -> none  [the longest x14 9.32 us: on_device(): lax.map(local_block, (inputs_blocks, in_blocks, out_blocks, rate_blocks,...]
  transfers between devices with their start and end apart: 4 -> 4, of which waited for: 4 -> 2; matrix products, arithmetic and copies ran while one was open for 9% -> 0% of each run, Pallas kernels for 0% -> 47%
where the time goes in v1:
time: 120 us; the launch traced here: 119 us
  Pallas kernels  68 us (57%)
  starting transfers between devices  33.2 us (28%)
  waiting for transfers between devices  12.8 us (11%)
  local copies, waits for them, and re-layouts  2.29 us (2%)
  other arithmetic  1.96 us (2%)
    pallas_call x2, Pallas kernels, local_pairs(): pl.pallas_call(lambda *refs: local_kernel(first, *refs), grid=(1,), in_sp...  49.3 us
    all_to_all x1, starting transfers between devices, on_device(): got = lax.all_to_all(pieces, SEQ, 0, 0)  13.7 us
    all_to_all x1, waiting for transfers between devices, on_device(): reduced = lax.all_to_all(reduced, 'y', 0, 0)  11.1 us
    all_to_all x1, starting transfers between devices, on_device(): got = lax.all_to_all(scanned, SEQ, 0, 0)  9.23 us
    pallas_call x1, Pallas kernels, on_device(): pl.pallas_call(rest_kernel, grid=(steps,), in_specs=[piece, heads, heads,...  6.88 us
    all_to_all x1, starting transfers between devices, on_device(): reduced = lax.all_to_all(reduced, 'y', 0, 0)  6.83 us
    pallas_call x1, Pallas kernels, on_device(): pl.pallas_call(maps_kernel, grid=(steps,), in_specs=[pl.BlockSpec(memory_...  5.09 us
    pallas_call x1, Pallas kernels, on_device(): pl.pallas_call(state_kernel, out_shape=[shape(32, 40, DIM), shape(8, TOK)...  4.71 us
  transfers between devices with their start and end apart: 4, of which 2 were waited for; matrix products, arithmetic and copies ran while one was open for 0% of the time, Pallas kernels for 47%

profile of v1, /device:TPU:1, one launch (start us, length us, event | category | flops | bytes accessed | tf_op | source)
XLA Modules:
  0.0 118.9 jit_solution(4647913716410671081)
XLA Ops:
  0.6 4.7 %states.1 = (f32[32,40,128]{2,1,0:T(8,128)}, f32[8,1024]{1,0:T(8,128)}) custom-call(bf16[1024,512]{1,0:T(8,128)(2,1)} %x_ref.5, bf16[1024,512]{1,0:T(8,128)(2,1)} %dy_ref.5, bf16[1024,128]{1,0:T(8,128)(2,1)} %b_ref.3, bf16[1024,128]{1,0:T(8,128)(2,1)} %c_ref.3, f32[4,1024]{1,0:T(4,128)} %refs_4_.3), custom_call_target="tpu_custom_call" | custom-call | tf_op jit(solution)/shard_map/states/pallas_call | solution.py:256
  5.3 13.7 %all-to-all-start = ((f32[32,40,128]{2,1,0:T(8,128)}), f32[32,40,128]{2,1,0:T(8,128)S(1)}, u32[]{:S(2)}, u32[]{:S(2)}) async-start(f32[32,40,128]{2,1,0:T(8,128)} %get-tuple-element.27), calls=%async_computation | async-start | bytes 1310720 | tf_op jit(solution)/shard_map/all_to_all | solution.py:262
  19.1 24.6 %local_0.1 = (f32[1024,256]{1,0:T(8,128)}, f32[1024,256]{1,0:T(8,128)}, f32[8,8,128]{2,1,0:T(8,128)}, f32[1024,128]{1,0:T(8,128)}) custom-call(bf16[1024,512]{1,0:T(8,128)(2,1)} %x_ref.5, bf16[1024,512]{1,0:T(8,128)(2,1)} %dy_ref.5, bf16[1024,128]{1,0:T(8,128)(2,1)} %b_ref.3, bf16[1024,128]{1,0:T(8,128)(2,1)} %c_ref.3, f32[4,1024]{1,0:T(4,128)} %refs_4_.3, ...), custom_call_target="tpu_custom_call" | custom-call | tf_op jit(solution)/shard_map/local_0/pallas_call | solution.py:243
  43.6 0.0 all-to-all-done.got_ref
  43.6 0.0 copy-start.1
  43.6 0.9 copy-done.1
  44.5 2.0 %scan.1 = f32[32,32,128]{2,1,0:T(8,128)} custom-call(f32[32,40,128]{2,1,0:T(8,128)} %copy-done.1), custom_call_target="tpu_custom_call" | custom-call | tf_op jit(solution)/shard_map/scan/pallas_call | solution.py:265
  46.5 9.2 %all-to-all-start.1 = ((f32[32,32,128]{2,1,0:T(8,128)}), f32[32,32,128]{2,1,0:T(8,128)S(1)}, u32[]{:S(2)}, u32[]{:S(2)}) async-start(f32[32,32,128]{2,1,0:T(8,128)} %scan.1), calls=%async_computation.1 | async-start | bytes 1048576 | tf_op jit(solution)/shard_map/all_to_all | solution.py:269
  55.7 24.8 %local_2.1 = (f32[1024,256]{1,0:T(8,128)}, f32[1024,256]{1,0:T(8,128)}, f32[8,8,128]{2,1,0:T(8,128)}) custom-call(bf16[1024,512]{1,0:T(8,128)(2,1)} %x_ref.5, bf16[1024,512]{1,0:T(8,128)(2,1)} %dy_ref.5, bf16[1024,128]{1,0:T(8,128)(2,1)} %b_ref.3, bf16[1024,128]{1,0:T(8,128)(2,1)} %c_ref.3, f32[4,1024]{1,0:T(4,128)} %refs_4_.3, ...), custom_call_target="tpu_custom_call" | custom-call | tf_op jit(solution)/shard_map/local_2/pallas_call | solution.py:243
  80.5 0.0 all-to-all-done.1.got_ref
  80.5 0.0 copy-start
  80.5 0.8 copy-done
  81.3 5.1 %maps.1 = (f32[8,64,256]{2,1,0:T(8,128)}, f32[8,64,256]{2,1,0:T(8,128)}) custom-call(s32[1]{0:T(128)} %bitcast.core_ref, f32[32,32,128]{2,1,0:T(8,128)} %copy-done, bf16[1024,512]{1,0:T(8,128)(2,1)} %x_ref.5, bf16[1024,512]{1,0:T(8,128)(2,1)} %dy_ref.5, f32[1024,128]{1,0:T(8,128)} %get-tuple-element.36.cols_ref, f32[1024,256]{1,0:T(8,128)} %get-tuple-element.37.local_ref), custom_call_target="tpu_custom_call" | custom-call | tf_op jit(solution)/shard_map/maps/pallas_call | solution.py:281
  86.4 3.4 %collective-permute-start = (f32[8,64,256]{2,1,0:T(8,128)}, f32[8,64,256]{2,1,0:T(8,128)S(1)}, u32[]{:S(2)}, u32[]{:S(2)}) collective-permute-start(f32[8,64,256]{2,1,0:T(8,128)} %get-tuple-element.39), channel_id=1, source_target_pairs={{0,1},{1,0},{2,3},{3,2},{4,5},{5,4},{6,7},{7,6},{8,9},{9,8},{10,11... | collective-permute-start | bytes 1572872 | tf_op jit(solution)/shard_map/ppermute | solution.py:291
  89.8 1.7 %collective-permute-done = f32[8,64,256]{2,1,0:T(8,128)S(1)} collective-permute-done((f32[8,64,256]{2,1,0:T(8,128)}, f32[8,64,256]{2,1,0:T(8,128)S(1)}, u32[]{:S(2)}, u32[]{:S(2)}) %collective-permute-start) | collective-permute-done | bytes 524320 | tf_op jit(solution)/shard_map/ppermute | solution.py:291
  91.5 1.9 %add.3 = f32[8,64,256]{2,1,0:T(8,128)} add(f32[8,64,256]{2,1,0:T(8,128)} %get-tuple-element.38, f32[8,64,256]{2,1,0:T(8,128)S(1)} %collective-permute-done) | non-fusion elementwise | flops 131072 | bytes 1572864 | tf_op jit(solution)/shard_map/add | solution.py:291
  93.4 6.8 %all-to-all-start.2 = ((f32[8,64,256]{2,1,0:T(8,128)}), f32[8,64,256]{2,1,0:T(8,128)S(1)}, u32[]{:S(2)}, u32[]{:S(2)}) async-start(f32[8,64,256]{2,1,0:T(8,128)} %add.3), calls=%async_computation.2 | async-start | bytes 1048576 | tf_op jit(solution)/shard_map/all_to_all | solution.py:293
  100.3 6.9 %rest.1 = (f32[1024,512]{1,0:T(8,128)}, f32[4,1024]{1,0:T(4,128)}) custom-call(f32[32,32,128]{2,1,0:T(8,128)} %copy-done, bf16[1024,512]{1,0:T(8,128)(2,1)} %x_ref.5, bf16[1024,512]{1,0:T(8,128)(2,1)} %dy_ref.5, bf16[1024,128]{1,0:T(8,128)(2,1)} %b_ref.3, bf16[1024,128]{1,0:T(8,128)(2,1)} %c_ref.3, f32[1024,128]{1,0:T(8,128)} %get-tuple-element.36.cols_ref, ...), custom_call_target="tpu_custom_call" | custom-call | tf_op jit(solution)/shard_map/rest/pallas_call | solution.py:294
  107.2 11.1 %all-to-all-done.2 = f32[8,64,256]{2,1,0:T(8,128)S(1)} async-done(((f32[8,64,256]{2,1,0:T(8,128)}), f32[8,64,256]{2,1,0:T(8,128)S(1)}, u32[]{:S(2)}, u32[]{:S(2)}) %all-to-all-start.2) | async-done | bytes 524320 | tf_op jit(solution)/shard_map/all_to_all | solution.py:293
  118.3 0.6 fusion
  (1 shorter events, 0.0 us)
Async XLA Ops:
  5.3 38.3 %all-to-all-start = ((f32[32,40,128]{2,1,0:T(8,128)}), f32[32,40,128]{2,1,0:T(8,128)S(1)}, u32[]{:S(2)}, u32[]{:S(2)}) async-start(f32[32,40,128]{2,1,0:T(8,128)} %get-tuple-element.27), calls=%async_computation | async-start | bytes 1310720 | tf_op jit(solution)/shard_map/all_to_all | solution.py:262
  43.6 0.9 copy-start.1
  46.5 34.0 %all-to-all-start.1 = ((f32[32,32,128]{2,1,0:T(8,128)}), f32[32,32,128]{2,1,0:T(8,128)S(1)}, u32[]{:S(2)}, u32[]{:S(2)}) async-start(f32[32,32,128]{2,1,0:T(8,128)} %scan.1), calls=%async_computation.1 | async-start | bytes 1048576 | tf_op jit(solution)/shard_map/all_to_all | solution.py:269
  80.5 0.8 copy-start
  86.4 5.1 %collective-permute-start = (f32[8,64,256]{2,1,0:T(8,128)}, f32[8,64,256]{2,1,0:T(8,128)S(1)}, u32[]{:S(2)}, u32[]{:S(2)}) collective-permute-start(f32[8,64,256]{2,1,0:T(8,128)} %get-tuple-element.39), channel_id=1, source_target_pairs={{0,1},{1,0},{2,3},{3,2},{4,5},{5,4},{6,7},{7,6},{8,9},{9,8},{10,11... | collective-permute-start | bytes 1572872 | tf_op jit(solution)/shard_map/ppermute | solution.py:291
  93.4 24.8 %all-to-all-start.2 = ((f32[8,64,256]{2,1,0:T(8,128)}), f32[8,64,256]{2,1,0:T(8,128)S(1)}, u32[]{:S(2)}, u32[]{:S(2)}) async-start(f32[8,64,256]{2,1,0:T(8,128)} %add.3), calls=%async_computation.2 | async-start | bytes 1048576 | tf_op jit(solution)/shard_map/all_to_all | solution.py:293

commit v2 on v1

v2 whole, which is shorter than its diff:
```python
import jax
import jax.numpy as jnp
from jax import lax
from jax.experimental import pallas as pl
from jax.experimental.pallas import tpu as pltpu
from jax.sharding import Mesh, PartitionSpec as P

f32, bf16 = jnp.float32, jnp.bfloat16
SEQ, HEAD = ("x", "z"), ("y", "core")
TOK, HEADS, DIM, TILE = 1024, 4, 128, 128
BLOCKS = TOK // TILE
STATES, LOCAL, SCAN, MAPS, REST = 56, 24, 4, 12, 16


def dot(a, b, dims):
    return lax.dot_general(a, b, (dims, ((), ())), preferred_element_type=f32)


def split(v):
    hi = v.astype(bf16)
    return hi, (v - hi.astype(f32)).astype(bf16)


def dot_wide(wide, exact):
    return dot(jnp.concatenate(split(wide), axis=1), jnp.concatenate([exact, exact], axis=0), ((1,), (0,)))


def running_sums(v, width, shift_suffix=True):
    lanes = v.shape[1]
    at = lax.broadcasted_iota(jnp.int32, v.shape, 1) & (width - 1)
    prefix = v
    suffix = jnp.where(at < width - 1, pltpu.roll(v, lanes - 1, 1), 0.0) if shift_suffix else v
    step = 1
    while step < width:
        prefix = prefix + jnp.where(at >= step, pltpu.roll(prefix, step, 1), 0.0)
        suffix = suffix + jnp.where(at < width - step, pltpu.roll(suffix, lanes - step, 1), 0.0)
        step *= 2
    return prefix, suffix


def state_kernel(x_ref, dy_ref, b_ref, c_ref, rate_ref, piece_ref, rows_ref, turned, total):
    step = pl.program_id(0)

    @pl.when(step == 0)
    def _():
        rates = jnp.concatenate([rate_ref[...], rate_ref[...]], axis=0)
        prefix, suffix = running_sums(rates, TOK)
        row = lax.broadcasted_iota(jnp.int32, rates.shape, 0)
        rows_ref[...] = jnp.exp(jnp.where(row < HEADS, suffix, prefix))
        totals = jnp.broadcast_to(jnp.exp(prefix[:, TOK - 1 :]), (8, DIM))
        total[0] = totals
        total[1] = jnp.concatenate([totals[2:], totals[:2]], axis=0)
        turned[0] = b_ref[...].astype(f32).T
        turned[1] = c_ref[...].astype(f32).T

    for k in range(16):
        piece_ref[k, 0, 32:40, :] = total[step]
    for h in range(2):
        for d, ref in enumerate((x_ref, dy_ref)):
            scaled = turned[d] * rows_ref[pl.ds(d * HEADS + 2 * step + h, 1), :]
            both = dot(jnp.concatenate(split(scaled), axis=0), ref[:, h * DIM : (h + 1) * DIM], ((1,), (0,)))
            state = both[:DIM] + both[DIM:]
            at = (d * 2 + h) * 8
            for k in range(16):
                piece_ref[k, 0, at : at + 8, :] = state[8 * k : 8 * k + 8]


def scan_kernel(got_ref, out_ref):
    for d in range(2):

        @pl.when(pl.program_id(0) == d)
        def _():
            for half in range(2):
                at = half * 8
                held = jnp.zeros((8, DIM), f32)
                for k in range(32) if d == 0 else reversed(range(32)):
                    out_ref[k, at : at + 8, :] = held
                    part = got_ref[k, d * 16 + at : d * 16 + at + 8, :]
                    held = held * got_ref[k, 32 + half : 33 + half, :] + part


def piece_of(got_ref, d, h):
    at = (d * 2 + h % 2) * 8
    return jnp.concatenate([got_ref[2 * k + h // 2, at : at + 8, :] for k in range(16)], axis=0)


def block_sums(rate_ref, rb, sb, tb):
    rates = jnp.concatenate([rate_ref[...], rate_ref[...]], axis=0)
    prefix, suffix = running_sums(rates, TILE)
    for k in range(BLOCKS):
        rb[k] = prefix[:, k * TILE : (k + 1) * TILE]
        sb[k] = suffix[:, k * TILE : (k + 1) * TILE]
        if tb is not None:
            tb[k] = jnp.broadcast_to(jnp.exp(prefix[:, (k + 1) * TILE - 1 : (k + 1) * TILE]), (8, TILE))


def local_kernel(x_ref, dy_ref, b_ref, c_ref, rate_ref, rows_ref, gx_ref, work_ref, decay_ref,
                 rb, sb, tb, ro, part, held_ref):
    block_sums(rate_ref, rb, sb, tb)
    causal = lax.broadcasted_iota(jnp.int32, (TILE, TILE), 0) <= lax.broadcasted_iota(jnp.int32, (TILE, TILE), 1)

    def block(j, nothing):
        at = pl.ds(pl.multiple_of(j * TILE, TILE), TILE)
        b, c, own = b_ref[at, :], c_ref[at, :], rb[j]
        scores = dot(b, c, ((1,), (1,)))
        scales = (jnp.exp(sb[j]), jnp.exp(own))
        turned = (b.astype(f32).T, c.astype(f32).T)
        joint = None
        for h in range(HEADS):
            lanes = slice(h * DIM, (h + 1) * DIM)
            x, dy = x_ref[at, lanes], dy_ref[at, lanes]
            across = jnp.broadcast_to(own[h : h + 1], (TILE, TILE))
            decay = jnp.where(causal, jnp.exp(across - across.T), 0.0)
            pairs = dot(x, dy, ((1,), (1,)))
            weights = decay * scores
            mine = decay * pairs
            joint = mine if joint is None else joint + mine
            product = weights * pairs
            gx_ref[at, lanes] = dot_wide(weights, dy)
            decay_ref[j, h : h + 1, :] = jnp.sum(product.T - product, axis=0, keepdims=True)
            for d, from_ in enumerate((x, dy)):
                wide = jnp.concatenate(split(turned[d] * scales[d][h : h + 1]), axis=0)
                both = dot(wide, from_, ((1,), (0,)))
                part[j, d * HEADS + h] = both[:DIM] + both[DIM:]
        work_ref[at, :DIM] = dot_wide(joint, c)
        work_ref[at, DIM : 2 * DIM] = dot_wide(joint.T, b)
        return nothing

    lax.fori_loop(0, BLOCKS, block, 0)
    for d in range(2):
        for h in range(HEADS):
            held = jnp.zeros((TILE, DIM), f32)
            for k in range(BLOCKS) if d == 0 else reversed(range(BLOCKS)):
                held_ref[k, d * HEADS + h] = jnp.concatenate(split(held), axis=1)
                held = held * tb[k, h : h + 1, :] + part[k, d * HEADS + h]
    for k in range(BLOCKS):
        ro[k] = rows_ref[:, k * TILE : (k + 1) * TILE]

    def carried(j, nothing):
        at = pl.ds(pl.multiple_of(j * TILE, TILE), TILE)
        b, c = b_ref[at, :], c_ref[at, :]
        wide_b, wide_c = b.astype(f32), c.astype(f32)
        scale = jnp.concatenate([jnp.exp(sb[j, 0:HEADS, :]), jnp.exp(rb[j, 0:HEADS, :])], axis=0)
        cols = jnp.concatenate([scale, ro[j]] * 8, axis=0).T
        work_ref[at, 2 * DIM :] = cols
        grad_in, grad_out = work_ref[at, :DIM], work_ref[at, DIM : 2 * DIM]
        for h in range(HEADS):
            lanes = slice(h * DIM, (h + 1) * DIM)
            after = held_ref[j, HEADS + h]
            to_end = jnp.broadcast_to(cols[:, h : h + 1], (TILE, DIM))
            stacked = jnp.concatenate([after[:, :DIM], after[:, DIM:]], axis=0)
            gx_ref[at, lanes] += to_end * dot(twice(b), stacked, ((1,), (0,)))
            fed_in = to_end * dot(twice(x_ref[at, lanes]), after, ((1,), (1,)))
            fed_out = cols[:, HEADS + h : HEADS + h + 1] * dot(twice(dy_ref[at, lanes]), held_ref[j, h], ((1,), (1,)))
            grad_in = grad_in + fed_in
            grad_out = grad_out + fed_out
            change = fed_in * wide_b - fed_out * wide_c
            decay_ref[j, h : h + 1, :] += jnp.sum(change.T, axis=0, keepdims=True)
        work_ref[at, :DIM] = grad_in
        work_ref[at, DIM : 2 * DIM] = grad_out
        return nothing

    lax.fori_loop(0, BLOCKS, carried, 0)


def twice(v):
    return jnp.concatenate([v, v], axis=1)


def maps_kernel(core_ref, got_ref, x_ref, dy_ref, work_ref, keep_ref, send_ref, parts):
    @pl.when(pl.program_id(0) == 0)
    def _():
        for d in range(2):
            for h in range(HEADS):
                parts[d * HEADS + h] = jnp.concatenate(split(piece_of(got_ref, d, h)), axis=1)

    grads = []
    for d, ref in ((1, x_ref), (0, dy_ref)):
        total = work_ref[:, (1 - d) * DIM : (2 - d) * DIM]
        for h in range(HEADS):
            at = 2 * DIM + 8 + (1 - d) * HEADS + h
            fed = dot(twice(ref[:, h * DIM : (h + 1) * DIM]), parts[d * HEADS + h], ((1,), (1,)))
            total = total + work_ref[:, at : at + 1] * fed
        grads.append(total)
    for core in range(2):
        for there in (core, 1 - core):
            out = keep_ref if there == core else send_ref

            @pl.when(core_ref[0] == core)
            def _():
                for k in range(out.shape[0]):
                    at = (2 * k + there) * 64
                    out[k, :, :DIM] = grads[0][at : at + 64]
                    out[k, :, DIM:] = grads[1][at : at + 64]


def rest_kernel(got_ref, x_ref, dy_ref, b_ref, c_ref, cols_ref, rows_ref, gx0_ref, decay0_ref,
                gx_ref, decay_ref, parts, stacked, sums):
    step = pl.program_id(0)
    tile = x_ref.shape[0]

    @pl.when(step == 0)
    def _():
        for h in range(HEADS):
            for d in range(2):
                parts[d * HEADS + h] = jnp.concatenate(split(piece_of(got_ref, d, h)), axis=1)
            stacked[h] = jnp.concatenate(split(piece_of(got_ref, 1, h)), axis=0)

    b, c = b_ref[...], c_ref[...]
    wide_b, wide_c = b.astype(f32), c.astype(f32)
    for h in range(HEADS):
        lanes = slice(h * DIM, (h + 1) * DIM)
        gx_ref[:, lanes] = gx0_ref[:, lanes] + cols_ref[:, 8 + h : 9 + h] * dot(twice(b), stacked[h], ((1,), (0,)))
        fed = dot(twice(x_ref[:, lanes]), parts[HEADS + h], ((1,), (1,))) * wide_b
        sums[step, h : h + 1, :] = jnp.sum(fed.T, axis=0, keepdims=True)
        fed = dot(twice(dy_ref[:, lanes]), parts[h], ((1,), (1,))) * wide_c
        sums[step, HEADS + h : HEADS + h + 1, :] = jnp.sum(fed.T, axis=0, keepdims=True)

    @pl.when(step == TOK // tile - 1)
    def _():
        rows = rows_ref[...]
        terms = jnp.concatenate([sums[k] for k in range(TOK // tile)], axis=1) * rows
        local = jnp.concatenate([decay0_ref[k, 0:HEADS, :] for k in range(BLOCKS)], axis=1)
        terms = terms + jnp.concatenate([local, jnp.zeros((HEADS, TOK), f32)], axis=0)
        at = lax.broadcasted_iota(jnp.int32, terms.shape, 1)
        moved = jnp.where(at >= 1, pltpu.roll(terms, 1, 1), 0.0)
        prefix, _ = running_sums(moved, TOK, False)
        _, suffix = running_sums(terms, TOK, False)
        decay = prefix[:HEADS] + suffix[HEADS:]
        which = lax.broadcasted_iota(jnp.int32, (HEADS, 1), 0)
        crossing = jnp.zeros((HEADS, 1), f32)
        for h in range(HEADS):
            both = jnp.sum(piece_of(got_ref, 0, h) * piece_of(got_ref, 1, h), axis=0, keepdims=True)
            both = jnp.sum(both, axis=1, keepdims=True)
            crossing = jnp.where(which == h, both, crossing)
        decay_ref[...] = decay + crossing * rows[HEADS:, TOK - 1 :]


def sum_kernel(parts_ref, in_ref, out_ref):
    total = parts_ref[0]
    for k in range(1, parts_ref.shape[0]):
        total = total + parts_ref[k]
    in_ref[...] = total[:, :DIM]
    out_ref[...] = total[:, DIM:]


def params(mib):
    return pltpu.CompilerParams(vmem_limit_bytes=mib << 20)


def shape(*dims, dtype=f32):
    return jax.ShapeDtypeStruct(dims, dtype)


def whole(*dims):
    return pl.BlockSpec(dims, lambda *_: (0,) * len(dims))


def on_device(inputs, in_map, out_map, log_decay, cotangent):
    half = pl.BlockSpec((TOK, 2 * DIM), lambda i: (0, i))
    pieces, rows = pl.pallas_call(
        state_kernel,
        grid=(2,),
        in_specs=[half, half, whole(TOK, DIM), whole(TOK, DIM), whole(HEADS, TOK)],
        out_specs=[pl.BlockSpec((16, 1, 40, DIM), lambda i: (0, i, 0, 0)), whole(8, TOK)],
        out_shape=[shape(16, 2, 40, DIM), shape(8, TOK)],
        scratch_shapes=[pltpu.VMEM((2, DIM, TOK), f32), pltpu.VMEM((2, 8, DIM), f32)],
        compiler_params=params(STATES),
        name="states",
    )(inputs, cotangent, in_map, out_map, log_decay)
    got = lax.all_to_all(pieces.reshape(32, 40, DIM), SEQ, 0, 0)
    sums = pltpu.VMEM((BLOCKS, 8, TILE), f32)
    gx, work, decay = pl.pallas_call(
        local_kernel,
        out_shape=[shape(TOK, HEADS * DIM), shape(TOK, 3 * DIM), shape(BLOCKS, 8, TILE)],
        scratch_shapes=[sums] * 4
        + [pltpu.VMEM((BLOCKS, 2 * HEADS, DIM, DIM), f32), pltpu.VMEM((BLOCKS, 2 * HEADS, DIM, 2 * DIM), bf16)],
        compiler_params=params(LOCAL),
        name="local",
    )(inputs, cotangent, in_map, out_map, log_decay, rows)
    got, work = lax.optimization_barrier((got, work))
    scanned = pl.pallas_call(
        scan_kernel,
        grid=(2,),
        in_specs=[whole(32, 40, DIM)],
        out_specs=pl.BlockSpec((32, 16, DIM), lambda i: (0, i, 0)),
        out_shape=pltpu.HBM((32, 32, DIM), f32),
        compiler_params=params(SCAN),
        name="scan",
    )(got)
    got = lax.all_to_all(scanned, SEQ, 0, 0)
    tile = 256
    steps = TOK // tile
    parts = pltpu.VMEM((2 * HEADS, DIM, 2 * DIM), bf16)
    heads = pl.BlockSpec((tile, HEADS * DIM), lambda i: (i, 0))
    one = pl.BlockSpec((tile, DIM), lambda i: (i, 0))
    piece = whole(32, 32, DIM)
    core = lax.axis_index("core").astype(jnp.int32).reshape(1)
    rows_of = pl.BlockSpec((steps // 2, 64, 2 * DIM), lambda i: (i, 0, 0))
    keep, send = pl.pallas_call(
        maps_kernel,
        grid=(steps,),
        in_specs=[pl.BlockSpec(memory_space=pltpu.SMEM), piece, heads, heads, pl.BlockSpec((tile, 3 * DIM), lambda i: (i, 0))],
        out_specs=[rows_of, rows_of],
        out_shape=[shape(8, 64, 2 * DIM)] * 2,
        scratch_shapes=[parts],
        compiler_params=params(MAPS),
        name="maps",
    )(core, got, inputs, cotangent, pltpu.with_memory_space_constraint(work, pltpu.HBM))
    reduced = keep + lax.ppermute(send, "core", [(0, 1), (1, 0)])
    reduced, got = lax.optimization_barrier((reduced, got))
    reduced = lax.all_to_all(reduced, "y", 0, 0)
    grad_inputs, grad_decay = pl.pallas_call(
        rest_kernel,
        grid=(steps,),
        in_specs=[
            piece, heads, heads, one, one, pl.BlockSpec((tile, DIM), lambda i: (i, 2)), whole(8, TOK), heads,
            whole(BLOCKS, 8, TILE),
        ],
        out_specs=[heads, whole(HEADS, TOK)],
        out_shape=[shape(TOK, HEADS * DIM), shape(HEADS, TOK)],
        scratch_shapes=[parts, pltpu.VMEM((HEADS, 2 * DIM, DIM), bf16), pltpu.VMEM((steps, 8, tile), f32)],
        compiler_params=params(REST),
        name="rest",
    )(got, inputs, cotangent, in_map, out_map, work, rows, gx, decay)
    reduced, grad_decay = lax.optimization_barrier((reduced, grad_decay))
    grad_in_map, grad_out_map = pl.pallas_call(
        sum_kernel, out_shape=[shape(64, DIM)] * 2, compiler_params=params(SCAN), name="sum"
    )(reduced)
    return (grad_inputs, grad_in_map, grad_out_map, grad_decay)


def solution(mesh):
    grid = Mesh(mesh.devices.reshape(4, 8, 8, 2), SEQ + HEAD)
    rows, columns = P(SEQ, None), P(SEQ, HEAD)
    return jax.shard_map(
        on_device,
        mesh=grid,
        in_specs=(columns, rows, rows, P(HEAD, SEQ), columns),
        out_specs=(columns, P(SEQ + HEAD, None), P(SEQ + HEAD, None), P(HEAD, SEQ)),
        check_vma=False,
    )
```

time: 120 us -> 97.9 us (0.82)
  Pallas kernels: 68 us -> 25.7 us
  waiting for transfers between devices: 12.8 us -> 28.3 us
  local copies, waits for them, and re-layouts: 2.29 us -> 6.25 us
  starting transfers between devices: 33.2 us -> 35.3 us
    pallas_call x4, Pallas kernels: 56 us -> 17.7 us  [the longest x1 10.6 us: on_device(): pl.pallas_call(local_kernel, out_shape=[shape(TOK, HEADS * DIM), shape(TO...]
    all_to_all x1, waiting for transfers between devices: 0.01 us -> 13.7 us  [on_device(): got = lax.all_to_all(scanned, SEQ, 0, 0)]
    unnamed x4 -> x22, local copies, waits for them, and re-layouts: 1.66 us -> 6.25 us
    ppermute x1, starting transfers between devices: 3.4 us -> 6.43 us  [on_device(): reduced = keep + lax.ppermute(send, 'core', [(0, 1), (1, 0)])]
    pallas_call x1, Pallas kernels: 6.88 us -> 4.43 us  [on_device(): pl.pallas_call(rest_kernel, grid=(steps,), in_specs=[piece, heads, heads,...]
    all_to_all x1, waiting for transfers between devices: 0.01 us -> 2.43 us  [on_device(): got = lax.all_to_all(pieces.reshape(32, 40, DIM), SEQ, 0, 0)]
    pallas_call x1, Pallas kernels: 5.09 us -> 3.59 us  [on_device(): pl.pallas_call(maps_kernel, grid=(steps,), in_specs=[pl.BlockSpec(memory_...]
  transfers between devices with their start and end apart: 4 -> 4, of which waited for: 2 -> 4; matrix products, arithmetic and copies ran while one was open for 0% -> 0% of each run, Pallas kernels for 47% -> 16%
where the time goes in v2:
time: 97.9 us; the launch traced here: 97.2 us
  starting transfers between devices  35.3 us (36%)
  waiting for transfers between devices  28.3 us (29%)
  Pallas kernels  25.7 us (26%)
  local copies, waits for them, and re-layouts  6.25 us (6%)
    all_to_all x1, waiting for transfers between devices, on_device(): got = lax.all_to_all(scanned, SEQ, 0, 0)  13.7 us
    all_to_all x1, starting transfers between devices, on_device(): got = lax.all_to_all(pieces.reshape(32, 40, DIM), SEQ, 0, 0)  13.7 us
    pallas_call x1, Pallas kernels, on_device(): pl.pallas_call(local_kernel, out_shape=[shape(TOK, HEADS * DIM), shape(TO...  10.6 us
    all_to_all x1, waiting for transfers between devices, on_device(): reduced = lax.all_to_all(reduced, 'y', 0, 0)  10.6 us
    all_to_all x1, starting transfers between devices, on_device(): got = lax.all_to_all(scanned, SEQ, 0, 0)  8.4 us
    all_to_all x1, starting transfers between devices, on_device(): reduced = lax.all_to_all(reduced, 'y', 0, 0)  6.8 us
    ppermute x1, starting transfers between devices, on_device(): reduced = keep + lax.ppermute(send, 'core', [(0, 1), (1, 0)])  6.43 us
    unnamed x22, local copies, waits for them, and re-layouts  6.25 us
  transfers between devices with their start and end apart: 4, of which 4 were waited for; matrix products, arithmetic and copies ran while one was open for 0% of the time, Pallas kernels for 16%

profile of v2, /device:TPU:1, one launch (start us, length us, event | category | flops | bytes accessed | tf_op | source)
XLA Modules:
  0.0 97.2 jit_solution(274936690478979101)
XLA Ops:
  0.6 0.0 copy-start.1
  0.6 0.0 copy-start
  0.7 0.0 copy-start.5
  0.7 0.0 copy-start.4
  0.7 0.0 copy-start.10
  0.7 4.4 %states.1 = (f32[16,2,40,128]{3,2,1,0:T(8,128)}, f32[8,1024]{1,0:T(8,128)}) custom-call(bf16[1024,512]{1,0:T(8,128)(2,1)} %x_ref.7, bf16[1024,512]{1,0:T(8,128)(2,1)} %dy_ref.7, bf16[1024,128]{1,0:T(8,128)(2,1)} %b_ref.5, bf16[1024,128]{1,0:T(8,128)(2,1)} %c_ref.5, f32[4,1024]{1,0:T(4,128)} %rate_ref.3), custom_call_target="tpu_custom_call" | custom-call | tf_op jit(solution)/shard_map/states/pallas_call | solution.py:261
  5.1 13.7 %all-to-all-start = ((f32[32,40,128]{2,1,0:T(8,128)}), f32[32,40,128]{2,1,0:T(8,128)S(1)}, u32[]{:S(2)}, u32[]{:S(2)}) async-start(f32[32,40,128]{2,1,0:T(8,128)} %bitcast.2), calls=%async_computation | async-start | bytes 1310720 | tf_op jit(solution)/shard_map/all_to_all | solution.py:271
  18.8 0.0 copy-done.1
  18.8 0.0 copy-done
  18.8 0.0 copy-done.5
  18.9 0.0 copy-done.4
  18.9 0.0 copy-done.10
  18.9 0.0 copy-start.8
  18.9 0.7 copy-done.8
  19.6 10.6 %local.1 = (f32[1024,512]{1,0:T(8,128)S(1)}, f32[1024,384]{1,0:T(8,128)S(1)}, f32[8,8,128]{2,1,0:T(8,128)S(1)}) custom-call(bf16[1024,512]{1,0:T(8,128)(2,1)S(1)} %copy-done, bf16[1024,512]{1,0:T(8,128)(2,1)S(1)} %copy-done.1, bf16[1024,128]{1,0:T(8,128)(2,1)S(1)} %copy-done.4, bf16[1024,128]{1,0:T(8,128)(2,1)S(1)} %copy-done.5, f32[4,1024]{1,0:T(4,128)S(1)} %copy-done.10, ...), custom_call_target="tpu_custom_call" | custom-call | tf_op jit(solution)/shard_map/local/pallas_call | solution.py:273
  30.3 0.0 copy-start.2
  30.3 1.2 %copy-done.2 = f32[1024,384]{1,0:T(8,128)} copy-done((f32[1024,384]{1,0:T(8,128)}, f32[1024,384]{1,0:T(8,128)S(1)}, u32[]{:S(2)}) %copy-start.2) | copy-done | bytes 1572888
  31.5 0.0 copy-start.6
  31.5 1.3 %copy-done.6 = f32[1024,512]{1,0:T(8,128)} copy-done((f32[1024,512]{1,0:T(8,128)}, f32[1024,512]{1,0:T(8,128)S(1)}, u32[]{:S(2)}) %copy-start.6) | copy-done | bytes 2097176
  32.8 2.4 %all-to-all-done.got_ref = f32[32,40,128]{2,1,0:T(8,128)S(1)} async-done(((f32[32,40,128]{2,1,0:T(8,128)}), f32[32,40,128]{2,1,0:T(8,128)S(1)}, u32[]{:S(2)}, u32[]{:S(2)}) %all-to-all-start) | async-done | bytes 655392 | tf_op jit(solution)/shard_map/all_to_all | solution.py:271
  35.2 0.9 scan.1
  36.1 8.4 %all-to-all-start.1 = ((f32[32,32,128]{2,1,0:T(8,128)}), f32[32,32,128]{2,1,0:T(8,128)S(1)}, u32[]{:S(2)}, u32[]{:S(2)}) async-start(f32[32,32,128]{2,1,0:T(8,128)} %scan.1), calls=%async_computation.1 | async-start | bytes 1048576 | tf_op jit(solution)/shard_map/all_to_all | solution.py:291
  44.5 13.7 %all-to-all-done.1.got_ref = f32[32,32,128]{2,1,0:T(8,128)S(1)} async-done(((f32[32,32,128]{2,1,0:T(8,128)}), f32[32,32,128]{2,1,0:T(8,128)S(1)}, u32[]{:S(2)}, u32[]{:S(2)}) %all-to-all-start.1) | async-done | bytes 524320 | tf_op jit(solution)/shard_map/all_to_all | solution.py:291
  58.3 3.6 %maps.1 = (f32[8,64,256]{2,1,0:T(8,128)S(1)}, f32[8,64,256]{2,1,0:T(8,128)S(1)}) custom-call(s32[1]{0:T(128)} %bitcast.core_ref, f32[32,32,128]{2,1,0:T(8,128)S(1)} %all-to-all-done.1.got_ref, bf16[1024,512]{1,0:T(8,128)(2,1)S(1)} %copy-done, bf16[1024,512]{1,0:T(8,128)(2,1)S(1)} %copy-done.1, f32[1024,384]{1,0:T(8,128)} %copy-done.2), custom_call_target="tpu_custom_call" | custom-call | tf_op jit(solution)/shard_map/maps/pallas_call | solution.py:300
  61.9 0.0 copy-start.9
  61.9 6.4 %collective-permute-start = (f32[8,64,256]{2,1,0:T(8,128)S(1)}, f32[8,64,256]{2,1,0:T(8,128)S(1)}, u32[]{:S(2)}, u32[]{:S(2)}) collective-permute-start(f32[8,64,256]{2,1,0:T(8,128)S(1)} %get-tuple-element.27), channel_id=1, source_target_pairs={{0,1},{1,0},{2,3},{3,2},{4,5},{5,4},{6,7},{7,6},{8,9},{9,8},{10,11... | collective-permute-start | bytes 1572872 | tf_op jit(solution)/shard_map/ppermute | solution.py:310
  68.3 1.5 %collective-permute-done = f32[8,64,256]{2,1,0:T(8,128)S(1)} collective-permute-done((f32[8,64,256]{2,1,0:T(8,128)S(1)}, f32[8,64,256]{2,1,0:T(8,128)S(1)}, u32[]{:S(2)}, u32[]{:S(2)}) %collective-permute-start) | collective-permute-done | bytes 524320 | tf_op jit(solution)/shard_map/ppermute | solution.py:310
  69.8 0.9 add.3
  70.7 6.8 %all-to-all-start.2 = ((f32[8,64,256]{2,1,0:T(8,128)}), f32[8,64,256]{2,1,0:T(8,128)}, u32[]{:S(2)}, u32[]{:S(2)}) async-start(f32[8,64,256]{2,1,0:T(8,128)} %add.3), calls=%async_computation.2 | async-start | bytes 1048576 | tf_op jit(solution)/shard_map/all_to_all | solution.py:312
  77.5 0.0 copy-done.9
  77.5 0.0 copy-start.3
  77.5 1.4 %copy-done.3 = f32[1024,384]{1,0:T(8,128)S(1)} copy-done((f32[1024,384]{1,0:T(8,128)S(1)}, f32[1024,384]{1,0:T(8,128)}, u32[]{:S(2)}) %copy-start.3) | copy-done | bytes 1572888
  78.9 0.0 copy-start.7
  78.9 1.6 %copy-done.7 = f32[1024,512]{1,0:T(8,128)S(1)} copy-done((f32[1024,512]{1,0:T(8,128)S(1)}, f32[1024,512]{1,0:T(8,128)}, u32[]{:S(2)}) %copy-start.7) | copy-done | bytes 2097176
  80.5 4.4 %rest.1 = (f32[1024,512]{1,0:T(8,128)}, f32[4,1024]{1,0:T(4,128)}) custom-call(f32[32,32,128]{2,1,0:T(8,128)S(1)} %all-to-all-done.1.got_ref, bf16[1024,512]{1,0:T(8,128)(2,1)S(1)} %copy-done, bf16[1024,512]{1,0:T(8,128)(2,1)S(1)} %copy-done.1, bf16[1024,128]{1,0:T(8,128)(2,1)S(1)} %copy-done.4, bf16[1024,128]{1,0:T(8,128)(2,1)S(1)} %copy-done.5, ...), custom_call_target="tpu_custom_call" | custom-call | tf_op jit(solution)/shard_map/rest/pallas_call | solution.py:313
  84.9 10.6 %all-to-all-done.2.parts_ref = f32[8,64,256]{2,1,0:T(8,128)} async-done(((f32[8,64,256]{2,1,0:T(8,128)}), f32[8,64,256]{2,1,0:T(8,128)}, u32[]{:S(2)}, u32[]{:S(2)}) %all-to-all-start.2) | async-done | bytes 524320 | tf_op jit(solution)/shard_map/all_to_all | solution.py:312
  95.5 1.7 %sum.1 = (f32[64,128]{1,0:T(8,128)}, f32[64,128]{1,0:T(8,128)}) custom-call(f32[8,64,256]{2,1,0:T(8,128)} %all-to-all-done.2.parts_ref), custom_call_target="tpu_custom_call" | custom-call | tf_op jit(solution)/shard_map/sum/pallas_call | solution.py:327
Async XLA Ops:
  0.6 18.2 %copy-start.1 = (bf16[1024,512]{1,0:T(8,128)(2,1)S(1)}, bf16[1024,512]{1,0:T(8,128)(2,1)}, u32[]{:S(2)}) copy-start(bf16[1024,512]{1,0:T(8,128)(2,1)} %dy_ref.7) | copy-start | bytes 3145732
  0.6 18.2 %copy-start = (bf16[1024,512]{1,0:T(8,128)(2,1)S(1)}, bf16[1024,512]{1,0:T(8,128)(2,1)}, u32[]{:S(2)}) copy-start(bf16[1024,512]{1,0:T(8,128)(2,1)} %x_ref.7) | copy-start | bytes 3145732
  0.7 18.2 %copy-start.5 = (bf16[1024,128]{1,0:T(8,128)(2,1)S(1)}, bf16[1024,128]{1,0:T(8,128)(2,1)}, u32[]{:S(2)}) copy-start(bf16[1024,128]{1,0:T(8,128)(2,1)} %c_ref.5) | copy-start | bytes 786436
  0.7 18.2 %copy-start.4 = (bf16[1024,128]{1,0:T(8,128)(2,1)S(1)}, bf16[1024,128]{1,0:T(8,128)(2,1)}, u32[]{:S(2)}) copy-start(bf16[1024,128]{1,0:T(8,128)(2,1)} %b_ref.5) | copy-start | bytes 786436
  0.7 18.2 %copy-start.10 = (f32[4,1024]{1,0:T(4,128)S(1)}, f32[4,1024]{1,0:T(4,128)}, u32[]{:S(2)}) copy-start(f32[4,1024]{1,0:T(4,128)} %rate_ref.3) | copy-start | bytes 49156
  5.1 30.1 %all-to-all-start = ((f32[32,40,128]{2,1,0:T(8,128)}), f32[32,40,128]{2,1,0:T(8,128)S(1)}, u32[]{:S(2)}, u32[]{:S(2)}) async-start(f32[32,40,128]{2,1,0:T(8,128)} %bitcast.2), calls=%async_computation | async-start | bytes 1310720 | tf_op jit(solution)/shard_map/all_to_all | solution.py:271
  18.9 0.8 copy-start.8
  30.3 1.2 %copy-start.2 = (f32[1024,384]{1,0:T(8,128)}, f32[1024,384]{1,0:T(8,128)S(1)}, u32[]{:S(2)}) copy-start(f32[1024,384]{1,0:T(8,128)S(1)} %get-tuple-element.25.work_ref.cols_ref) | copy-start | bytes 4718596
  31.5 1.3 %copy-start.6 = (f32[1024,512]{1,0:T(8,128)}, f32[1024,512]{1,0:T(8,128)S(1)}, u32[]{:S(2)}) copy-start(f32[1024,512]{1,0:T(8,128)S(1)} %get-tuple-element.29.gx0_ref) | copy-start | bytes 6291460
  36.1 22.2 %all-to-all-start.1 = ((f32[32,32,128]{2,1,0:T(8,128)}), f32[32,32,128]{2,1,0:T(8,128)S(1)}, u32[]{:S(2)}, u32[]{:S(2)}) async-start(f32[32,32,128]{2,1,0:T(8,128)} %scan.1), calls=%async_computation.1 | async-start | bytes 1048576 | tf_op jit(solution)/shard_map/all_to_all | solution.py:291
  61.9 15.6 %copy-start.9 = (f32[8,1024]{1,0:T(8,128)S(1)}, f32[8,1024]{1,0:T(8,128)}, u32[]{:S(2)}) copy-start(f32[8,1024]{1,0:T(8,128)} %get-tuple-element.22.rows_ref) | copy-start | bytes 98308
  61.9 7.9 %collective-permute-start = (f32[8,64,256]{2,1,0:T(8,128)S(1)}, f32[8,64,256]{2,1,0:T(8,128)S(1)}, u32[]{:S(2)}, u32[]{:S(2)}) collective-permute-start(f32[8,64,256]{2,1,0:T(8,128)S(1)} %get-tuple-element.27), channel_id=1, source_target_pairs={{0,1},{1,0},{2,3},{3,2},{4,5},{5,4},{6,7},{7,6},{8,9},{9,8},{10,11... | collective-permute-start | bytes 1572872 | tf_op jit(solution)/shard_map/ppermute | solution.py:310
  70.7 24.9 %all-to-all-start.2 = ((f32[8,64,256]{2,1,0:T(8,128)}), f32[8,64,256]{2,1,0:T(8,128)}, u32[]{:S(2)}, u32[]{:S(2)}) async-start(f32[8,64,256]{2,1,0:T(8,128)} %add.3), calls=%async_computation.2 | async-start | bytes 1048576 | tf_op jit(solution)/shard_map/all_to_all | solution.py:312
  77.5 1.4 %copy-start.3 = (f32[1024,384]{1,0:T(8,128)S(1)}, f32[1024,384]{1,0:T(8,128)}, u32[]{:S(2)}) copy-start(f32[1024,384]{1,0:T(8,128)} %copy-done.2) | copy-start | bytes 4718596
  78.9 1.6 %copy-start.7 = (f32[1024,512]{1,0:T(8,128)S(1)}, f32[1024,512]{1,0:T(8,128)}, u32[]{:S(2)}) copy-start(f32[1024,512]{1,0:T(8,128)} %copy-done.6) | copy-start | bytes 6291460

commit v3 on v2

--- a/solution.py
+++ b/solution.py
@@ -9,7 +9,7 @@
 SEQ, HEAD = ("x", "z"), ("y", "core")
 TOK, HEADS, DIM, TILE = 1024, 4, 128, 128
 BLOCKS = TOK // TILE
-STATES, LOCAL, SCAN, MAPS, REST = 56, 24, 4, 12, 16
+STATES, LOCAL, SCAN, MAPS, REST = 56, 24, 4, 12, 10
 
 
 def dot(a, b, dims):
@@ -84,6 +84,17 @@
     return jnp.concatenate([got_ref[2 * k + h // 2, at : at + 8, :] for k in range(16)], axis=0)
 
 
+def columns(rows):
+    return jnp.concatenate([jnp.concatenate([rows[:, k : k + TILE]] * 16, axis=0).T for k in range(0, rows.shape[1], TILE)], axis=0)
+
+
+def sort_rows(core_ref, rows_ref, keep_ref, send_ref):
+    own = pl.multiple_of(core_ref[0] * 64, 64)
+    for k in range(keep_ref.shape[0]):
+        keep_ref[k] = rows_ref[pl.ds(k * 128 + own, 64), :]
+        send_ref[k] = rows_ref[pl.ds(k * 128 + 64 - own, 64), :]
+
+
 def block_sums(rate_ref, rb, sb, tb):
     rates = jnp.concatenate([rate_ref[...], rate_ref[...]], axis=0)
     prefix, suffix = running_sums(rates, TILE)
@@ -94,8 +105,8 @@
             tb[k] = jnp.broadcast_to(jnp.exp(prefix[:, (k + 1) * TILE - 1 : (k + 1) * TILE]), (8, TILE))
 
 
-def local_kernel(x_ref, dy_ref, b_ref, c_ref, rate_ref, rows_ref, gx_ref, work_ref, decay_ref,
-                 rb, sb, tb, ro, part, held_ref):
+def local_kernel(core_ref, x_ref, dy_ref, b_ref, c_ref, rate_ref, gx_ref, keep_ref, send_ref, decay_ref,
+                 rb, sb, tb, part, held_ref, work_ref):
     block_sums(rate_ref, rb, sb, tb)
     causal = lax.broadcasted_iota(jnp.int32, (TILE, TILE), 0) <= lax.broadcasted_iota(jnp.int32, (TILE, TILE), 1)
 
@@ -133,16 +144,12 @@
             for k in range(BLOCKS) if d == 0 else reversed(range(BLOCKS)):
                 held_ref[k, d * HEADS + h] = jnp.concatenate(split(held), axis=1)
                 held = held * tb[k, h : h + 1, :] + part[k, d * HEADS + h]
-    for k in range(BLOCKS):
-        ro[k] = rows_ref[:, k * TILE : (k + 1) * TILE]
-
     def carried(j, nothing):
         at = pl.ds(pl.multiple_of(j * TILE, TILE), TILE)
         b, c = b_ref[at, :], c_ref[at, :]
         wide_b, wide_c = b.astype(f32), c.astype(f32)
         scale = jnp.concatenate([jnp.exp(sb[j, 0:HEADS, :]), jnp.exp(rb[j, 0:HEADS, :])], axis=0)
-        cols = jnp.concatenate([scale, ro[j]] * 8, axis=0).T
-        work_ref[at, 2 * DIM :] = cols
+        cols = columns(scale)
         grad_in, grad_out = work_ref[at, :DIM], work_ref[at, DIM : 2 * DIM]
         for h in range(HEADS):
             lanes = slice(h * DIM, (h + 1) * DIM)
@@ -161,40 +168,33 @@
         return nothing
 
     lax.fori_loop(0, BLOCKS, carried, 0)
+    sort_rows(core_ref, work_ref, keep_ref, send_ref)
 
 
 def twice(v):
     return jnp.concatenate([v, v], axis=1)
 
 
-def maps_kernel(core_ref, got_ref, x_ref, dy_ref, work_ref, keep_ref, send_ref, parts):
+def maps_kernel(core_ref, got_ref, x_ref, dy_ref, rows_ref, keep_ref, send_ref, parts, work):
     @pl.when(pl.program_id(0) == 0)
     def _():
         for d in range(2):
             for h in range(HEADS):
                 parts[d * HEADS + h] = jnp.concatenate(split(piece_of(got_ref, d, h)), axis=1)
 
-    grads = []
+    cols = columns(rows_ref[...])
     for d, ref in ((1, x_ref), (0, dy_ref)):
-        total = work_ref[:, (1 - d) * DIM : (2 - d) * DIM]
-        for h in range(HEADS):
-            at = 2 * DIM + 8 + (1 - d) * HEADS + h
+        total = None
+        for h in range(HEADS):
+            at = (1 - d) * HEADS + h
             fed = dot(twice(ref[:, h * DIM : (h + 1) * DIM]), parts[d * HEADS + h], ((1,), (1,)))
-            total = total + work_ref[:, at : at + 1] * fed
-        grads.append(total)
-    for core in range(2):
-        for there in (core, 1 - core):
-            out = keep_ref if there == core else send_ref
-
-            @pl.when(core_ref[0] == core)
-            def _():
-                for k in range(out.shape[0]):
-                    at = (2 * k + there) * 64
-                    out[k, :, :DIM] = grads[0][at : at + 64]
-                    out[k, :, DIM:] = grads[1][at : at + 64]
-
-
-def rest_kernel(got_ref, x_ref, dy_ref, b_ref, c_ref, cols_ref, rows_ref, gx0_ref, decay0_ref,
+            fed = cols[:, at : at + 1] * fed
+            total = fed if total is None else total + fed
+        work[:, (1 - d) * DIM : (2 - d) * DIM] = total
+    sort_rows(core_ref, work, keep_ref, send_ref)
+
+
+def rest_kernel(got_ref, x_ref, dy_ref, b_ref, c_ref, tile_rows_ref, rows_ref, gx0_ref, decay0_ref,
                 gx_ref, decay_ref, parts, stacked, sums):
     step = pl.program_id(0)
     tile = x_ref.shape[0]
@@ -208,9 +208,10 @@
 
     b, c = b_ref[...], c_ref[...]
     wide_b, wide_c = b.astype(f32), c.astype(f32)
+    cols = columns(tile_rows_ref[...])
     for h in range(HEADS):
         lanes = slice(h * DIM, (h + 1) * DIM)
-        gx_ref[:, lanes] = gx0_ref[:, lanes] + cols_ref[:, 8 + h : 9 + h] * dot(twice(b), stacked[h], ((1,), (0,)))
+        gx_ref[:, lanes] = gx0_ref[:, lanes] + cols[:, h : h + 1] * dot(twice(b), stacked[h], ((1,), (0,)))
         fed = dot(twice(x_ref[:, lanes]), parts[HEADS + h], ((1,), (1,))) * wide_b
         sums[step, h : h + 1, :] = jnp.sum(fed.T, axis=0, keepdims=True)
         fed = dot(twice(dy_ref[:, lanes]), parts[h], ((1,), (1,))) * wide_c
@@ -270,15 +271,23 @@
     )(inputs, cotangent, in_map, out_map, log_decay)
     got = lax.all_to_all(pieces.reshape(32, 40, DIM), SEQ, 0, 0)
     sums = pltpu.VMEM((BLOCKS, 8, TILE), f32)
-    gx, work, decay = pl.pallas_call(
+    core = lax.axis_index("core").astype(jnp.int32).reshape(1)
+    scalar = pl.BlockSpec(memory_space=pltpu.SMEM)
+    sorted_rows = shape(8, 64, 2 * DIM)
+    gx, keep_near, send_near, decay = pl.pallas_call(
         local_kernel,
-        out_shape=[shape(TOK, HEADS * DIM), shape(TOK, 3 * DIM), shape(BLOCKS, 8, TILE)],
-        scratch_shapes=[sums] * 4
-        + [pltpu.VMEM((BLOCKS, 2 * HEADS, DIM, DIM), f32), pltpu.VMEM((BLOCKS, 2 * HEADS, DIM, 2 * DIM), bf16)],
+        in_specs=[scalar] + [whole(*v.shape) for v in (inputs, cotangent, in_map, out_map, log_decay)],
+        out_shape=[shape(TOK, HEADS * DIM), sorted_rows, sorted_rows, shape(BLOCKS, 8, TILE)],
+        scratch_shapes=[sums] * 3
+        + [
+            pltpu.VMEM((BLOCKS, 2 * HEADS, DIM, DIM), f32),
+            pltpu.VMEM((BLOCKS, 2 * HEADS, DIM, 2 * DIM), bf16),
+            pltpu.VMEM((TOK, 2 * DIM), f32),
+        ],
         compiler_params=params(LOCAL),
         name="local",
-    )(inputs, cotangent, in_map, out_map, log_decay, rows)
-    got, work = lax.optimization_barrier((got, work))
+    )(core, inputs, cotangent, in_map, out_map, log_decay)
+    got, send_near = lax.optimization_barrier((got, send_near))
     scanned = pl.pallas_call(
         scan_kernel,
         grid=(2,),
@@ -288,33 +297,37 @@
         compiler_params=params(SCAN),
         name="scan",
     )(got)
+    scanned, send_near = lax.optimization_barrier((scanned, send_near))
     got = lax.all_to_all(scanned, SEQ, 0, 0)
+    swap = [(0, 1), (1, 0)]
+    near = keep_near + lax.ppermute(send_near, "core", swap)
+    got, near = lax.optimization_barrier((got, near))
     tile = 256
     steps = TOK // tile
     parts = pltpu.VMEM((2 * HEADS, DIM, 2 * DIM), bf16)
     heads = pl.BlockSpec((tile, HEADS * DIM), lambda i: (i, 0))
     one = pl.BlockSpec((tile, DIM), lambda i: (i, 0))
     piece = whole(32, 32, DIM)
-    core = lax.axis_index("core").astype(jnp.int32).reshape(1)
+    tile_rows = pl.BlockSpec((8, tile), lambda i: (0, i))
     rows_of = pl.BlockSpec((steps // 2, 64, 2 * DIM), lambda i: (i, 0, 0))
     keep, send = pl.pallas_call(
         maps_kernel,
         grid=(steps,),
-        in_specs=[pl.BlockSpec(memory_space=pltpu.SMEM), piece, heads, heads, pl.BlockSpec((tile, 3 * DIM), lambda i: (i, 0))],
+        in_specs=[scalar, piece, heads, heads, tile_rows],
         out_specs=[rows_of, rows_of],
-        out_shape=[shape(8, 64, 2 * DIM)] * 2,
-        scratch_shapes=[parts],
+        out_shape=[sorted_rows] * 2,
+        scratch_shapes=[parts, pltpu.VMEM((tile, 2 * DIM), f32)],
         compiler_params=params(MAPS),
         name="maps",
-    )(core, got, inputs, cotangent, pltpu.with_memory_space_constraint(work, pltpu.HBM))
-    reduced = keep + lax.ppermute(send, "core", [(0, 1), (1, 0)])
+    )(core, got, inputs, cotangent, rows)
+    reduced = keep + near + lax.ppermute(send, "core", swap)
     reduced, got = lax.optimization_barrier((reduced, got))
     reduced = lax.all_to_all(reduced, "y", 0, 0)
     grad_inputs, grad_decay = pl.pallas_call(
         rest_kernel,
         grid=(steps,),
         in_specs=[
-            piece, heads, heads, one, one, pl.BlockSpec((tile, DIM), lambda i: (i, 2)), whole(8, TOK), heads,
+            piece, heads, heads, one, one, tile_rows, whole(8, TOK), heads,
             whole(BLOCKS, 8, TILE),
         ],
         out_specs=[heads, whole(HEADS, TOK)],
@@ -322,7 +335,7 @@
         scratch_shapes=[parts, pltpu.VMEM((HEADS, 2 * DIM, DIM), bf16), pltpu.VMEM((steps, 8, tile), f32)],
         compiler_params=params(REST),
         name="rest",
-    )(got, inputs, cotangent, in_map, out_map, work, rows, gx, decay)
+    )(got, inputs, cotangent, in_map, out_map, rows, rows, gx, decay)
     reduced, grad_decay = lax.optimization_barrier((reduced, grad_decay))
     grad_in_map, grad_out_map = pl.pallas_call(
         sum_kernel, out_shape=[shape(64, DIM)] * 2, compiler_params=params(SCAN), name="sum"

time: 97.9 us -> 96.3 us (0.984)
  starting transfers between devices: 35.3 us -> 38.8 us
  waiting for transfers between devices: 28.3 us -> 24.8 us
  other arithmetic: 0.86 us -> 2.82 us
  Pallas kernels: 25.7 us -> 24 us
  local copies, waits for them, and re-layouts: 6.25 us -> 4.56 us
    all_to_all x1, waiting for transfers between devices: 13.7 us -> 6.72 us  [on_device(): got = lax.all_to_all(scanned, SEQ, 0, 0)]
    ppermute x1 -> x2, starting transfers between devices: 6.43 us -> 9.82 us  [the longest x1 6.45 us: on_device(): reduced = keep + near + lax.ppermute(send, 'core', swap)]
    add x1 -> x2, other arithmetic: 0.86 us -> 2.82 us  [the longest x1 1.92 us: on_device(): near = keep_near + lax.ppermute(send_near, 'core', swap)]
    ppermute x1 -> x2, waiting for transfers between devices: 1.51 us -> 3.24 us  [the longest x1 1.73 us: on_device(): near = keep_near + lax.ppermute(send_near, 'core', swap)]
    unnamed x22, local copies, waits for them, and re-layouts: 6.25 us -> 4.56 us
    pallas_call x2, Pallas kernels: 14.2 us -> 12.7 us  [the longest x1 10.7 us: on_device(): pl.pallas_call(local_kernel, in_specs=[scalar] + [whole(*v.shape) for v i...]
    all_to_all x1, waiting for transfers between devices: 10.6 us -> 12.1 us  [on_device(): reduced = lax.all_to_all(reduced, 'y', 0, 0)]
  transfers between devices with their start and end apart: 4 -> 5, of which waited for: 4 -> 5; matrix products, arithmetic and copies ran while one was open for 0% -> 2% of each run, Pallas kernels for 16% -> 16%
where the time goes in v3:
time: 96.3 us; the launch traced here: 95.7 us
  starting transfers between devices  38.8 us (40%)
  waiting for transfers between devices  24.8 us (26%)
  Pallas kernels  24 us (25%)
  local copies, waits for them, and re-layouts  4.56 us (5%)
  other arithmetic  2.82 us (3%)
    all_to_all x1, starting transfers between devices, on_device(): got = lax.all_to_all(pieces.reshape(32, 40, DIM), SEQ, 0, 0)  13.7 us
    all_to_all x1, waiting for transfers between devices, on_device(): reduced = lax.all_to_all(reduced, 'y', 0, 0)  12.1 us
    pallas_call x1, Pallas kernels, on_device(): pl.pallas_call(local_kernel, in_specs=[scalar] + [whole(*v.shape) for v i...  10.7 us
    all_to_all x1, starting transfers between devices, on_device(): got = lax.all_to_all(scanned, SEQ, 0, 0)  8.4 us
    all_to_all x1, starting transfers between devices, on_device(): reduced = lax.all_to_all(reduced, 'y', 0, 0)  6.84 us
    all_to_all x1, waiting for transfers between devices, on_device(): got = lax.all_to_all(scanned, SEQ, 0, 0)  6.72 us
    ppermute x1, starting transfers between devices, on_device(): reduced = keep + near + lax.ppermute(send, 'core', swap)  6.45 us
    unnamed x22, local copies, waits for them, and re-layouts  4.56 us
  transfers between devices with their start and end apart: 5, of which 5 were waited for; matrix products, arithmetic and copies ran while one was open for 2% of the time, Pallas kernels for 16%

profile of v3, /device:TPU:1, one launch (start us, length us, event | category | flops | bytes accessed | tf_op | source)
XLA Modules:
  0.0 95.7 jit_solution(3003297179821148)
XLA Ops:
  0.6 0.0 copy-start.1
  0.6 0.0 copy-start
  0.7 0.0 copy-start.3
  0.7 0.0 copy-start.2
  0.7 0.0 copy-start.8
  0.7 4.4 %states.1 = (f32[16,2,40,128]{3,2,1,0:T(8,128)}, f32[8,1024]{1,0:T(8,128)}) custom-call(bf16[1024,512]{1,0:T(8,128)(2,1)} %x_ref.7, bf16[1024,512]{1,0:T(8,128)(2,1)} %dy_ref.7, bf16[1024,128]{1,0:T(8,128)(2,1)} %b_ref.5, bf16[1024,128]{1,0:T(8,128)(2,1)} %c_ref.5, f32[4,1024]{1,0:T(4,128)} %rate_ref.3), custom_call_target="tpu_custom_call" | custom-call | tf_op jit(solution)/shard_map/states/pallas_call | solution.py:262
  5.1 13.7 %all-to-all-start = ((f32[32,40,128]{2,1,0:T(8,128)}), f32[32,40,128]{2,1,0:T(8,128)S(1)}, u32[]{:S(2)}, u32[]{:S(2)}) async-start(f32[32,40,128]{2,1,0:T(8,128)} %bitcast.2), calls=%async_computation | async-start | bytes 1310720 | tf_op jit(solution)/shard_map/all_to_all | solution.py:272
  18.8 0.0 copy-done.1
  18.8 0.0 copy-done
  18.8 0.0 copy-done.3
  18.8 0.0 copy-done.2
  18.9 0.0 copy-done.8
  18.9 10.7 %local.1 = (f32[1024,512]{1,0:T(8,128)S(1)}, f32[8,64,256]{2,1,0:T(8,128)S(1)}, f32[8,64,256]{2,1,0:T(8,128)S(1)}, f32[8,8,128]{2,1,0:T(8,128)S(1)}) custom-call(s32[1]{0:T(128)} %bitcast.core_ref, bf16[1024,512]{1,0:T(8,128)(2,1)S(1)} %copy-done, bf16[1024,512]{1,0:T(8,128)(2,1)S(1)} %copy-done.1, bf16[1024,128]{1,0:T(8,128)(2,1)S(1)} %copy-done.2, ...), custom_call_target="tpu_custom_call" | custom-call | tf_op jit(solution)/shard_map/local/pallas_call | solution.py:277
  29.6 0.0 copy-start.4
  29.6 1.3 %copy-done.4 = f32[1024,512]{1,0:T(8,128)} copy-done((f32[1024,512]{1,0:T(8,128)}, f32[1024,512]{1,0:T(8,128)S(1)}, u32[]{:S(2)}) %copy-start.4) | copy-done | bytes 2097176
  30.9 0.0 copy-start.6
  30.9 0.8 copy-done.6
  31.7 0.0 copy-start.9
  31.7 0.8 copy-done.9
  32.5 0.0 copy-start.7
  32.5 2.7 %all-to-all-done.got_ref = f32[32,40,128]{2,1,0:T(8,128)S(1)} async-done(((f32[32,40,128]{2,1,0:T(8,128)}), f32[32,40,128]{2,1,0:T(8,128)S(1)}, u32[]{:S(2)}, u32[]{:S(2)}) %all-to-all-start) | async-done | bytes 655392 | tf_op jit(solution)/shard_map/all_to_all | solution.py:272
  35.2 0.9 scan.1
  36.1 8.4 %all-to-all-start.1 = ((f32[32,32,128]{2,1,0:T(8,128)}), f32[32,32,128]{2,1,0:T(8,128)S(1)}, u32[]{:S(2)}, u32[]{:S(2)}) async-start(f32[32,32,128]{2,1,0:T(8,128)} %scan.1), calls=%async_computation.1 | async-start | bytes 1048576 | tf_op jit(solution)/shard_map/all_to_all | solution.py:301
  44.5 3.4 %collective-permute-start = (f32[8,64,256]{2,1,0:T(8,128)}, f32[8,64,256]{2,1,0:T(8,128)S(1)}, u32[]{:S(2)}, u32[]{:S(2)}) collective-permute-start(f32[8,64,256]{2,1,0:T(8,128)} %copy-done.9), channel_id=1, source_target_pairs={{0,1},{1,0},{2,3},{3,2},{4,5},{5,4},{6,7},{7,6},{8,9},{9,8},{10,11... | collective-permute-start | bytes 1572872 | tf_op jit(solution)/shard_map/ppermute | solution.py:303
  47.9 1.7 %collective-permute-done = f32[8,64,256]{2,1,0:T(8,128)S(1)} collective-permute-done((f32[8,64,256]{2,1,0:T(8,128)}, f32[8,64,256]{2,1,0:T(8,128)S(1)}, u32[]{:S(2)}, u32[]{:S(2)}) %collective-permute-start) | collective-permute-done | bytes 524320 | tf_op jit(solution)/shard_map/ppermute | solution.py:303
  49.6 1.9 %add.9 = f32[8,64,256]{2,1,0:T(8,128)} add(f32[8,64,256]{2,1,0:T(8,128)} %copy-done.6, f32[8,64,256]{2,1,0:T(8,128)S(1)} %collective-permute-done) | non-fusion elementwise | flops 131072 | bytes 1572864 | tf_op jit(solution)/shard_map/add | solution.py:303
  51.5 6.7 %all-to-all-done.1.got_ref = f32[32,32,128]{2,1,0:T(8,128)S(1)} async-done(((f32[32,32,128]{2,1,0:T(8,128)}), f32[32,32,128]{2,1,0:T(8,128)S(1)}, u32[]{:S(2)}, u32[]{:S(2)}) %all-to-all-start.1) | async-done | bytes 524320 | tf_op jit(solution)/shard_map/all_to_all | solution.py:301
  58.2 0.0 copy-start.10
  58.2 0.0 copy-done.7
  58.2 2.0 %maps.1 = (f32[8,64,256]{2,1,0:T(8,128)S(1)}, f32[8,64,256]{2,1,0:T(8,128)S(1)}) custom-call(s32[1]{0:T(128)} %bitcast.core_ref, f32[32,32,128]{2,1,0:T(8,128)S(1)} %all-to-all-done.1.got_ref, bf16[1024,512]{1,0:T(8,128)(2,1)S(1)} %copy-done, bf16[1024,512]{1,0:T(8,128)(2,1)S(1)} %copy-done.1, f32[8,1024]{1,0:T(8,128)S(1)} %copy-done.7), custom_call_target="tpu_custom_call" | custom-call | tf_op jit(solution)/shard_map/maps/pallas_call | solution.py:313
  60.3 6.4 %collective-permute-start.1 = (f32[8,64,256]{2,1,0:T(8,128)S(1)}, f32[8,64,256]{2,1,0:T(8,128)S(1)}, u32[]{:S(2)}, u32[]{:S(2)}) collective-permute-start(f32[8,64,256]{2,1,0:T(8,128)S(1)} %get-tuple-element.37), channel_id=1, source_target_pairs={{0,1},{1,0},{2,3},{3,2},{4,5},{5,4},{6,7},{7,6},{8,9},{9,8},{10,11... | collective-permute-start | bytes 1572872 | tf_op jit(solution)/shard_map/ppermute | solution.py:323
  66.7 1.5 %collective-permute-done.1 = f32[8,64,256]{2,1,0:T(8,128)S(1)} collective-permute-done((f32[8,64,256]{2,1,0:T(8,128)S(1)}, f32[8,64,256]{2,1,0:T(8,128)S(1)}, u32[]{:S(2)}, u32[]{:S(2)}) %collective-permute-start.1) | collective-permute-done | bytes 524320 | tf_op jit(solution)/shard_map/ppermute | solution.py:323
  68.2 0.0 copy-done.10
  68.2 0.9 add_add_fusion
  69.1 6.8 %all-to-all-start.2 = ((f32[8,64,256]{2,1,0:T(8,128)}), f32[8,64,256]{2,1,0:T(8,128)}, u32[]{:S(2)}, u32[]{:S(2)}) async-start(f32[8,64,256]{2,1,0:T(8,128)} %add_add_fusion), calls=%async_computation.2 | async-start | bytes 1048576 | tf_op jit(solution)/shard_map/all_to_all | solution.py:325
  76.0 0.0 copy-start.5
  76.0 1.6 %copy-done.5 = f32[1024,512]{1,0:T(8,128)S(1)} copy-done((f32[1024,512]{1,0:T(8,128)S(1)}, f32[1024,512]{1,0:T(8,128)}, u32[]{:S(2)}) %copy-start.5) | copy-done | bytes 2097176
  77.6 4.3 %rest.1 = (f32[1024,512]{1,0:T(8,128)}, f32[4,1024]{1,0:T(4,128)}) custom-call(f32[32,32,128]{2,1,0:T(8,128)S(1)} %all-to-all-done.1.got_ref, bf16[1024,512]{1,0:T(8,128)(2,1)S(1)} %copy-done, bf16[1024,512]{1,0:T(8,128)(2,1)S(1)} %copy-done.1, bf16[1024,128]{1,0:T(8,128)(2,1)S(1)} %copy-done.2, bf16[1024,128]{1,0:T(8,128)(2,1)S(1)} %copy-done.3, ...), custom_call_target="tpu_custom_call" | custom-call | tf_op jit(solution)/shard_map/rest/pallas_call | solution.py:326
  81.9 12.1 %all-to-all-done.2.parts_ref = f32[8,64,256]{2,1,0:T(8,128)} async-done(((f32[8,64,256]{2,1,0:T(8,128)}), f32[8,64,256]{2,1,0:T(8,128)}, u32[]{:S(2)}, u32[]{:S(2)}) %all-to-all-start.2) | async-done | bytes 524320 | tf_op jit(solution)/shard_map/all_to_all | solution.py:325
  94.0 1.7 %sum.1 = (f32[64,128]{1,0:T(8,128)}, f32[64,128]{1,0:T(8,128)}) custom-call(f32[8,64,256]{2,1,0:T(8,128)} %all-to-all-done.2.parts_ref), custom_call_target="tpu_custom_call" | custom-call | tf_op jit(solution)/shard_map/sum/pallas_call | solution.py:340
Async XLA Ops:
  0.6 18.2 %copy-start.1 = (bf16[1024,512]{1,0:T(8,128)(2,1)S(1)}, bf16[1024,512]{1,0:T(8,128)(2,1)}, u32[]{:S(2)}) copy-start(bf16[1024,512]{1,0:T(8,128)(2,1)} %dy_ref.7) | copy-start | bytes 3145732
  0.6 18.2 %copy-start = (bf16[1024,512]{1,0:T(8,128)(2,1)S(1)}, bf16[1024,512]{1,0:T(8,128)(2,1)}, u32[]{:S(2)}) copy-start(bf16[1024,512]{1,0:T(8,128)(2,1)} %x_ref.7) | copy-start | bytes 3145732
  0.7 18.2 %copy-start.3 = (bf16[1024,128]{1,0:T(8,128)(2,1)S(1)}, bf16[1024,128]{1,0:T(8,128)(2,1)}, u32[]{:S(2)}) copy-start(bf16[1024,128]{1,0:T(8,128)(2,1)} %c_ref.5) | copy-start | bytes 786436
  0.7 18.2 %copy-start.2 = (bf16[1024,128]{1,0:T(8,128)(2,1)S(1)}, bf16[1024,128]{1,0:T(8,128)(2,1)}, u32[]{:S(2)}) copy-start(bf16[1024,128]{1,0:T(8,128)(2,1)} %b_ref.5) | copy-start | bytes 786436
  0.7 18.2 %copy-start.8 = (f32[4,1024]{1,0:T(4,128)S(1)}, f32[4,1024]{1,0:T(4,128)}, u32[]{:S(2)}) copy-start(f32[4,1024]{1,0:T(4,128)} %rate_ref.3) | copy-start | bytes 49156
  5.1 30.1 %all-to-all-start = ((f32[32,40,128]{2,1,0:T(8,128)}), f32[32,40,128]{2,1,0:T(8,128)S(1)}, u32[]{:S(2)}, u32[]{:S(2)}) async-start(f32[32,40,128]{2,1,0:T(8,128)} %bitcast.2), calls=%async_computation | async-start | bytes 1310720 | tf_op jit(solution)/shard_map/all_to_all | solution.py:272
  29.6 1.3 %copy-start.4 = (f32[1024,512]{1,0:T(8,128)}, f32[1024,512]{1,0:T(8,128)S(1)}, u32[]{:S(2)}) copy-start(f32[1024,512]{1,0:T(8,128)S(1)} %get-tuple-element.39.gx0_ref) | copy-start | bytes 6291460
  30.9 0.8 copy-start.6
  31.7 0.8 copy-start.9
  32.5 25.7 %copy-start.7 = (f32[8,1024]{1,0:T(8,128)S(1)}, f32[8,1024]{1,0:T(8,128)}, u32[]{:S(2)}) copy-start(f32[8,1024]{1,0:T(8,128)} %get-tuple-element.34.rows_ref.tile_rows_ref) | copy-start | bytes 98308
  36.1 22.2 %all-to-all-start.1 = ((f32[32,32,128]{2,1,0:T(8,128)}), f32[32,32,128]{2,1,0:T(8,128)S(1)}, u32[]{:S(2)}, u32[]{:S(2)}) async-start(f32[32,32,128]{2,1,0:T(8,128)} %scan.1), calls=%async_computation.1 | async-start | bytes 1048576 | tf_op jit(solution)/shard_map/all_to_all | solution.py:301
  44.5 5.1 %collective-permute-start = (f32[8,64,256]{2,1,0:T(8,128)}, f32[8,64,256]{2,1,0:T(8,128)S(1)}, u32[]{:S(2)}, u32[]{:S(2)}) collective-permute-start(f32[8,64,256]{2,1,0:T(8,128)} %copy-done.9), channel_id=1, source_target_pairs={{0,1},{1,0},{2,3},{3,2},{4,5},{5,4},{6,7},{7,6},{8,9},{9,8},{10,11... | collective-permute-start | bytes 1572872 | tf_op jit(solution)/shard_map/ppermute | solution.py:303
  58.2 10.0 %copy-start.10 = (f32[8,64,256]{2,1,0:T(8,128)S(1)}, f32[8,64,256]{2,1,0:T(8,128)}, u32[]{:S(2)}) copy-start(f32[8,64,256]{2,1,0:T(8,128)} %add.9) | copy-start | bytes 1572868
  60.3 8.0 %collective-permute-start.1 = (f32[8,64,256]{2,1,0:T(8,128)S(1)}, f32[8,64,256]{2,1,0:T(8,128)S(1)}, u32[]{:S(2)}, u32[]{:S(2)}) collective-permute-start(f32[8,64,256]{2,1,0:T(8,128)S(1)} %get-tuple-element.37), channel_id=1, source_target_pairs={{0,1},{1,0},{2,3},{3,2},{4,5},{5,4},{6,7},{7,6},{8,9},{9,8},{10,11... | collective-permute-start | bytes 1572872 | tf_op jit(solution)/shard_map/ppermute | solution.py:323
  69.1 24.9 %all-to-all-start.2 = ((f32[8,64,256]{2,1,0:T(8,128)}), f32[8,64,256]{2,1,0:T(8,128)}, u32[]{:S(2)}, u32[]{:S(2)}) async-start(f32[8,64,256]{2,1,0:T(8,128)} %add_add_fusion), calls=%async_computation.2 | async-start | bytes 1048576 | tf_op jit(solution)/shard_map/all_to_all | solution.py:325
  76.0 1.6 %copy-start.5 = (f32[1024,512]{1,0:T(8,128)S(1)}, f32[1024,512]{1,0:T(8,128)}, u32[]{:S(2)}) copy-start(f32[1024,512]{1,0:T(8,128)} %copy-done.4) | copy-start | bytes 6291460

commit v4 on v3

--- a/solution.py
+++ b/solution.py
@@ -54,15 +54,16 @@
         turned[1] = c_ref[...].astype(f32).T
 
     for k in range(16):
-        piece_ref[k, 0, 32:40, :] = total[step]
+        piece_ref[k, 0, 8] = total[step, 0:4, :]
     for h in range(2):
         for d, ref in enumerate((x_ref, dy_ref)):
             scaled = turned[d] * rows_ref[pl.ds(d * HEADS + 2 * step + h, 1), :]
             both = dot(jnp.concatenate(split(scaled), axis=0), ref[:, h * DIM : (h + 1) * DIM], ((1,), (0,)))
             state = both[:DIM] + both[DIM:]
-            at = (d * 2 + h) * 8
+            at = (d * 2 + h) * 2
             for k in range(16):
-                piece_ref[k, 0, at : at + 8, :] = state[8 * k : 8 * k + 8]
+                piece_ref[k, 0, at] = state[8 * k : 8 * k + 4]
+                piece_ref[k, 0, at + 1] = state[8 * k + 4 : 8 * k + 8]
 
 
 def scan_kernel(got_ref, out_ref):
@@ -70,13 +71,11 @@
 
         @pl.when(pl.program_id(0) == d)
         def _():
-            for half in range(2):
-                at = half * 8
-                held = jnp.zeros((8, DIM), f32)
+            for at in range(0, 16, 4):
+                held = jnp.zeros((4, DIM), f32)
                 for k in range(32) if d == 0 else reversed(range(32)):
-                    out_ref[k, at : at + 8, :] = held
-                    part = got_ref[k, d * 16 + at : d * 16 + at + 8, :]
-                    held = held * got_ref[k, 32 + half : 33 + half, :] + part
+                    out_ref[k, at : at + 4, :] = held
+                    held = held * got_ref[k, 8, at // 8 : at // 8 + 1, :] + got_ref[k, d * 4 + at // 4]
 
 
 def piece_of(got_ref, d, h):
@@ -263,13 +262,13 @@
         state_kernel,
         grid=(2,),
         in_specs=[half, half, whole(TOK, DIM), whole(TOK, DIM), whole(HEADS, TOK)],
-        out_specs=[pl.BlockSpec((16, 1, 40, DIM), lambda i: (0, i, 0, 0)), whole(8, TOK)],
-        out_shape=[shape(16, 2, 40, DIM), shape(8, TOK)],
+        out_specs=[pl.BlockSpec((16, 1, 9, 4, DIM), lambda i: (0, i, 0, 0, 0)), whole(8, TOK)],
+        out_shape=[shape(16, 2, 9, 4, DIM), shape(8, TOK)],
         scratch_shapes=[pltpu.VMEM((2, DIM, TOK), f32), pltpu.VMEM((2, 8, DIM), f32)],
         compiler_params=params(STATES),
         name="states",
     )(inputs, cotangent, in_map, out_map, log_decay)
-    got = lax.all_to_all(pieces.reshape(32, 40, DIM), SEQ, 0, 0)
+    got = lax.all_to_all(pieces.reshape(32, 9, 4, DIM), SEQ, 0, 0)
     sums = pltpu.VMEM((BLOCKS, 8, TILE), f32)
     core = lax.axis_index("core").astype(jnp.int32).reshape(1)
     scalar = pl.BlockSpec(memory_space=pltpu.SMEM)
@@ -291,7 +290,7 @@
     scanned = pl.pallas_call(
         scan_kernel,
         grid=(2,),
-        in_specs=[whole(32, 40, DIM)],
+        in_specs=[whole(32, 9, 4, DIM)],
         out_specs=pl.BlockSpec((32, 16, DIM), lambda i: (0, i, 0)),
         out_shape=pltpu.HBM((32, 32, DIM), f32),
         compiler_params=params(SCAN),

time: 96.3 us -> 94.6 us (0.982)
  waiting for transfers between devices: 24.8 us -> 23.6 us
    all_to_all x1, waiting for transfers between devices: 2.67 us -> 1.59 us  [on_device(): got = lax.all_to_all(pieces.reshape(32, 9, 4, DIM), SEQ, 0, 0)]
where the time goes in v4:
time: 94.6 us; the launch traced here: 94.1 us
  starting transfers between devices  38.2 us (40%)
  Pallas kernels  24.1 us (25%)
  waiting for transfers between devices  23.6 us (25%)
  local copies, waits for them, and re-layouts  4.54 us (5%)
  other arithmetic  2.81 us (3%)
    all_to_all x1, starting transfers between devices, on_device(): got = lax.all_to_all(pieces.reshape(32, 9, 4, DIM), SEQ, 0, 0)  13.7 us
    all_to_all x1, waiting for transfers between devices, on_device(): reduced = lax.all_to_all(reduced, 'y', 0, 0)  12.1 us
    pallas_call x1, Pallas kernels, on_device(): pl.pallas_call(local_kernel, in_specs=[scalar] + [whole(*v.shape) for v i...  10.7 us
    all_to_all x1, starting transfers between devices, on_device(): got = lax.all_to_all(scanned, SEQ, 0, 0)  8.04 us
    all_to_all x1, waiting for transfers between devices, on_device(): got = lax.all_to_all(scanned, SEQ, 0, 0)  6.66 us
    all_to_all x1, starting transfers between devices, on_device(): reduced = lax.all_to_all(reduced, 'y', 0, 0)  6.61 us
    ppermute x1, starting transfers between devices, on_device(): reduced = keep + near + lax.ppermute(send, 'core', swap)  6.42 us
    unnamed x22, local copies, waits for them, and re-layouts  4.54 us
  transfers between devices with their start and end apart: 5, of which 5 were waited for; matrix products, arithmetic and copies ran while one was open for 2% of the time, Pallas kernels for 16%

profile of v4, /device:TPU:1, one launch (start us, length us, event | category | flops | bytes accessed | tf_op | source)
XLA Modules:
  0.0 94.1 jit_solution(8003561419684777388)
XLA Ops:
  0.6 0.0 copy-start.1
  0.6 0.0 copy-start
  0.7 0.0 copy-start.3
  0.7 0.0 copy-start.2
  0.7 0.0 copy-start.8
  0.7 4.4 %states.1 = (f32[16,2,9,4,128]{4,3,2,1,0:T(4,128)}, f32[8,1024]{1,0:T(8,128)}) custom-call(bf16[1024,512]{1,0:T(8,128)(2,1)} %x_ref.7, bf16[1024,512]{1,0:T(8,128)(2,1)} %dy_ref.7, bf16[1024,128]{1,0:T(8,128)(2,1)} %b_ref.5, bf16[1024,128]{1,0:T(8,128)(2,1)} %c_ref.5, f32[4,1024]{1,0:T(4,128)} %rate_ref.3), custom_call_target="tpu_custom_call" | custom-call | tf_op jit(solution)/shard_map/states/pallas_call | solution.py:261
  5.1 13.7 %all-to-all-start = ((f32[32,9,4,128]{3,2,1,0:T(4,128)}), f32[32,9,4,128]{3,2,1,0:T(4,128)S(1)}, u32[]{:S(2)}, u32[]{:S(2)}) async-start(f32[32,9,4,128]{3,2,1,0:T(4,128)} %bitcast.2), calls=%async_computation | async-start | bytes 1179648 | tf_op jit(solution)/shard_map/all_to_all | solution.py:271
  18.9 0.0 copy-done.1
  18.9 0.0 copy-done
  18.9 0.0 copy-done.3
  18.9 0.0 copy-done.2
  18.9 0.0 copy-done.8
  18.9 10.7 %local.1 = (f32[1024,512]{1,0:T(8,128)S(1)}, f32[8,64,256]{2,1,0:T(8,128)S(1)}, f32[8,64,256]{2,1,0:T(8,128)S(1)}, f32[8,8,128]{2,1,0:T(8,128)S(1)}) custom-call(s32[1]{0:T(128)} %bitcast.core_ref, bf16[1024,512]{1,0:T(8,128)(2,1)S(1)} %copy-done, bf16[1024,512]{1,0:T(8,128)(2,1)S(1)} %copy-done.1, bf16[1024,128]{1,0:T(8,128)(2,1)S(1)} %copy-done.2, ...), custom_call_target="tpu_custom_call" | custom-call | tf_op jit(solution)/shard_map/local/pallas_call | solution.py:276
  29.6 0.0 copy-start.4
  29.6 1.3 %copy-done.4 = f32[1024,512]{1,0:T(8,128)} copy-done((f32[1024,512]{1,0:T(8,128)}, f32[1024,512]{1,0:T(8,128)S(1)}, u32[]{:S(2)}) %copy-start.4) | copy-done | bytes 2097176
  30.9 0.0 copy-start.6
  30.9 0.8 copy-done.6
  31.7 0.0 copy-start.9
  31.7 0.8 copy-done.9
  32.5 0.0 copy-start.7
  32.5 1.6 %all-to-all-done.got_ref = f32[32,9,4,128]{3,2,1,0:T(4,128)S(1)} async-done(((f32[32,9,4,128]{3,2,1,0:T(4,128)}), f32[32,9,4,128]{3,2,1,0:T(4,128)S(1)}, u32[]{:S(2)}, u32[]{:S(2)}) %all-to-all-start) | async-done | bytes 589856 | tf_op jit(solution)/shard_map/all_to_all | solution.py:271
  34.1 0.9 scan.1
  35.1 8.0 %all-to-all-start.1 = ((f32[32,32,128]{2,1,0:T(8,128)}), f32[32,32,128]{2,1,0:T(8,128)S(1)}, u32[]{:S(2)}, u32[]{:S(2)}) async-start(f32[32,32,128]{2,1,0:T(8,128)} %scan.1), calls=%async_computation.1 | async-start | bytes 1048576 | tf_op jit(solution)/shard_map/all_to_all | solution.py:300
  43.1 3.4 %collective-permute-start = (f32[8,64,256]{2,1,0:T(8,128)}, f32[8,64,256]{2,1,0:T(8,128)S(1)}, u32[]{:S(2)}, u32[]{:S(2)}) collective-permute-start(f32[8,64,256]{2,1,0:T(8,128)} %copy-done.9), channel_id=1, source_target_pairs={{0,1},{1,0},{2,3},{3,2},{4,5},{5,4},{6,7},{7,6},{8,9},{9,8},{10,11... | collective-permute-start | bytes 1572872 | tf_op jit(solution)/shard_map/ppermute | solution.py:302
  46.5 1.7 %collective-permute-done = f32[8,64,256]{2,1,0:T(8,128)S(1)} collective-permute-done((f32[8,64,256]{2,1,0:T(8,128)}, f32[8,64,256]{2,1,0:T(8,128)S(1)}, u32[]{:S(2)}, u32[]{:S(2)}) %collective-permute-start) | collective-permute-done | bytes 524320 | tf_op jit(solution)/shard_map/ppermute | solution.py:302
  48.3 1.9 %add.9 = f32[8,64,256]{2,1,0:T(8,128)} add(f32[8,64,256]{2,1,0:T(8,128)} %copy-done.6, f32[8,64,256]{2,1,0:T(8,128)S(1)} %collective-permute-done) | non-fusion elementwise | flops 131072 | bytes 1572864 | tf_op jit(solution)/shard_map/add | solution.py:302
  50.2 6.7 %all-to-all-done.1.got_ref = f32[32,32,128]{2,1,0:T(8,128)S(1)} async-done(((f32[32,32,128]{2,1,0:T(8,128)}), f32[32,32,128]{2,1,0:T(8,128)S(1)}, u32[]{:S(2)}, u32[]{:S(2)}) %all-to-all-start.1) | async-done | bytes 524320 | tf_op jit(solution)/shard_map/all_to_all | solution.py:300
  56.8 0.0 copy-start.10
  56.8 0.0 copy-done.7
  56.8 2.0 %maps.1 = (f32[8,64,256]{2,1,0:T(8,128)S(1)}, f32[8,64,256]{2,1,0:T(8,128)S(1)}) custom-call(s32[1]{0:T(128)} %bitcast.core_ref, f32[32,32,128]{2,1,0:T(8,128)S(1)} %all-to-all-done.1.got_ref, bf16[1024,512]{1,0:T(8,128)(2,1)S(1)} %copy-done, bf16[1024,512]{1,0:T(8,128)(2,1)S(1)} %copy-done.1, f32[8,1024]{1,0:T(8,128)S(1)} %copy-done.7), custom_call_target="tpu_custom_call" | custom-call | tf_op jit(solution)/shard_map/maps/pallas_call | solution.py:312
  58.9 6.4 %collective-permute-start.1 = (f32[8,64,256]{2,1,0:T(8,128)S(1)}, f32[8,64,256]{2,1,0:T(8,128)S(1)}, u32[]{:S(2)}, u32[]{:S(2)}) collective-permute-start(f32[8,64,256]{2,1,0:T(8,128)S(1)} %get-tuple-element.37), channel_id=1, source_target_pairs={{0,1},{1,0},{2,3},{3,2},{4,5},{5,4},{6,7},{7,6},{8,9},{9,8},{10,11... | collective-permute-start | bytes 1572872 | tf_op jit(solution)/shard_map/ppermute | solution.py:322
  65.3 1.5 %collective-permute-done.1 = f32[8,64,256]{2,1,0:T(8,128)S(1)} collective-permute-done((f32[8,64,256]{2,1,0:T(8,128)S(1)}, f32[8,64,256]{2,1,0:T(8,128)S(1)}, u32[]{:S(2)}, u32[]{:S(2)}) %collective-permute-start.1) | collective-permute-done | bytes 524320 | tf_op jit(solution)/shard_map/ppermute | solution.py:322
  66.8 0.0 copy-done.10
  66.8 0.9 add_add_fusion
  67.7 6.6 %all-to-all-start.2 = ((f32[8,64,256]{2,1,0:T(8,128)}), f32[8,64,256]{2,1,0:T(8,128)}, u32[]{:S(2)}, u32[]{:S(2)}) async-start(f32[8,64,256]{2,1,0:T(8,128)} %add_add_fusion), calls=%async_computation.2 | async-start | bytes 1048576 | tf_op jit(solution)/shard_map/all_to_all | solution.py:324
  74.3 0.0 copy-start.5
  74.3 1.6 %copy-done.5 = f32[1024,512]{1,0:T(8,128)S(1)} copy-done((f32[1024,512]{1,0:T(8,128)S(1)}, f32[1024,512]{1,0:T(8,128)}, u32[]{:S(2)}) %copy-start.5) | copy-done | bytes 2097176
  75.9 4.3 %rest.1 = (f32[1024,512]{1,0:T(8,128)}, f32[4,1024]{1,0:T(4,128)}) custom-call(f32[32,32,128]{2,1,0:T(8,128)S(1)} %all-to-all-done.1.got_ref, bf16[1024,512]{1,0:T(8,128)(2,1)S(1)} %copy-done, bf16[1024,512]{1,0:T(8,128)(2,1)S(1)} %copy-done.1, bf16[1024,128]{1,0:T(8,128)(2,1)S(1)} %copy-done.2, bf16[1024,128]{1,0:T(8,128)(2,1)S(1)} %copy-done.3, ...), custom_call_target="tpu_custom_call" | custom-call | tf_op jit(solution)/shard_map/rest/pallas_call | solution.py:325
  80.3 12.1 %all-to-all-done.2.parts_ref = f32[8,64,256]{2,1,0:T(8,128)} async-done(((f32[8,64,256]{2,1,0:T(8,128)}), f32[8,64,256]{2,1,0:T(8,128)}, u32[]{:S(2)}, u32[]{:S(2)}) %all-to-all-start.2) | async-done | bytes 524320 | tf_op jit(solution)/shard_map/all_to_all | solution.py:324
  92.4 1.7 %sum.1 = (f32[64,128]{1,0:T(8,128)}, f32[64,128]{1,0:T(8,128)}) custom-call(f32[8,64,256]{2,1,0:T(8,128)} %all-to-all-done.2.parts_ref), custom_call_target="tpu_custom_call" | custom-call | tf_op jit(solution)/shard_map/sum/pallas_call | solution.py:339
Async XLA Ops:
  0.6 18.2 %copy-start.1 = (bf16[1024,512]{1,0:T(8,128)(2,1)S(1)}, bf16[1024,512]{1,0:T(8,128)(2,1)}, u32[]{:S(2)}) copy-start(bf16[1024,512]{1,0:T(8,128)(2,1)} %dy_ref.7) | copy-start | bytes 3145732
  0.6 18.2 %copy-start = (bf16[1024,512]{1,0:T(8,128)(2,1)S(1)}, bf16[1024,512]{1,0:T(8,128)(2,1)}, u32[]{:S(2)}) copy-start(bf16[1024,512]{1,0:T(8,128)(2,1)} %x_ref.7) | copy-start | bytes 3145732
  0.7 18.2 %copy-start.3 = (bf16[1024,128]{1,0:T(8,128)(2,1)S(1)}, bf16[1024,128]{1,0:T(8,128)(2,1)}, u32[]{:S(2)}) copy-start(bf16[1024,128]{1,0:T(8,128)(2,1)} %c_ref.5) | copy-start | bytes 786436
  0.7 18.2 %copy-start.2 = (bf16[1024,128]{1,0:T(8,128)(2,1)S(1)}, bf16[1024,128]{1,0:T(8,128)(2,1)}, u32[]{:S(2)}) copy-start(bf16[1024,128]{1,0:T(8,128)(2,1)} %b_ref.5) | copy-start | bytes 786436
  0.7 18.2 %copy-start.8 = (f32[4,1024]{1,0:T(4,128)S(1)}, f32[4,1024]{1,0:T(4,128)}, u32[]{:S(2)}) copy-start(f32[4,1024]{1,0:T(4,128)} %rate_ref.3) | copy-start | bytes 49156
  5.1 29.0 %all-to-all-start = ((f32[32,9,4,128]{3,2,1,0:T(4,128)}), f32[32,9,4,128]{3,2,1,0:T(4,128)S(1)}, u32[]{:S(2)}, u32[]{:S(2)}) async-start(f32[32,9,4,128]{3,2,1,0:T(4,128)} %bitcast.2), calls=%async_computation | async-start | bytes 1179648 | tf_op jit(solution)/shard_map/all_to_all | solution.py:271
  29.6 1.3 %copy-start.4 = (f32[1024,512]{1,0:T(8,128)}, f32[1024,512]{1,0:T(8,128)S(1)}, u32[]{:S(2)}) copy-start(f32[1024,512]{1,0:T(8,128)S(1)} %get-tuple-element.39.gx0_ref) | copy-start | bytes 6291460
  30.9 0.8 copy-start.6
  31.7 0.8 copy-start.9
  32.5 24.3 %copy-start.7 = (f32[8,1024]{1,0:T(8,128)S(1)}, f32[8,1024]{1,0:T(8,128)}, u32[]{:S(2)}) copy-start(f32[8,1024]{1,0:T(8,128)} %get-tuple-element.34.rows_ref.tile_rows_ref) | copy-start | bytes 98308
  35.1 21.8 %all-to-all-start.1 = ((f32[32,32,128]{2,1,0:T(8,128)}), f32[32,32,128]{2,1,0:T(8,128)S(1)}, u32[]{:S(2)}, u32[]{:S(2)}) async-start(f32[32,32,128]{2,1,0:T(8,128)} %scan.1), calls=%async_computation.1 | async-start | bytes 1048576 | tf_op jit(solution)/shard_map/all_to_all | solution.py:300
  43.1 5.2 %collective-permute-start = (f32[8,64,256]{2,1,0:T(8,128)}, f32[8,64,256]{2,1,0:T(8,128)S(1)}, u32[]{:S(2)}, u32[]{:S(2)}) collective-permute-start(f32[8,64,256]{2,1,0:T(8,128)} %copy-done.9), channel_id=1, source_target_pairs={{0,1},{1,0},{2,3},{3,2},{4,5},{5,4},{6,7},{7,6},{8,9},{9,8},{10,11... | collective-permute-start | bytes 1572872 | tf_op jit(solution)/shard_map/ppermute | solution.py:302
  56.8 10.0 %copy-start.10 = (f32[8,64,256]{2,1,0:T(8,128)S(1)}, f32[8,64,256]{2,1,0:T(8,128)}, u32[]{:S(2)}) copy-start(f32[8,64,256]{2,1,0:T(8,128)} %add.9) | copy-start | bytes 1572868
  58.9 7.9 %collective-permute-start.1 = (f32[8,64,256]{2,1,0:T(8,128)S(1)}, f32[8,64,256]{2,1,0:T(8,128)S(1)}, u32[]{:S(2)}, u32[]{:S(2)}) collective-permute-start(f32[8,64,256]{2,1,0:T(8,128)S(1)} %get-tuple-element.37), channel_id=1, source_target_pairs={{0,1},{1,0},{2,3},{3,2},{4,5},{5,4},{6,7},{7,6},{8,9},{9,8},{10,11... | collective-permute-start | bytes 1572872 | tf_op jit(solution)/shard_map/ppermute | solution.py:322
  67.7 24.7 %all-to-all-start.2 = ((f32[8,64,256]{2,1,0:T(8,128)}), f32[8,64,256]{2,1,0:T(8,128)}, u32[]{:S(2)}, u32[]{:S(2)}) async-start(f32[8,64,256]{2,1,0:T(8,128)} %add_add_fusion), calls=%async_computation.2 | async-start | bytes 1048576 | tf_op jit(solution)/shard_map/all_to_all | solution.py:324
  74.3 1.6 %copy-start.5 = (f32[1024,512]{1,0:T(8,128)S(1)}, f32[1024,512]{1,0:T(8,128)}, u32[]{:S(2)}) copy-start(f32[1024,512]{1,0:T(8,128)} %copy-done.4) | copy-start | bytes 6291460

commit v5 on v4

--- a/solution.py
+++ b/solution.py
@@ -9,7 +9,7 @@
 SEQ, HEAD = ("x", "z"), ("y", "core")
 TOK, HEADS, DIM, TILE = 1024, 4, 128, 128
 BLOCKS = TOK // TILE
-STATES, LOCAL, SCAN, MAPS, REST = 56, 24, 4, 12, 10
+STATES, LOCAL, SCAN, MAPS, REST = 56, 24, 4, 12, 56
 
 
 def dot(a, b, dims):
@@ -308,14 +308,15 @@
     one = pl.BlockSpec((tile, DIM), lambda i: (i, 0))
     piece = whole(32, 32, DIM)
     tile_rows = pl.BlockSpec((8, tile), lambda i: (0, i))
-    rows_of = pl.BlockSpec((steps // 2, 64, 2 * DIM), lambda i: (i, 0, 0))
+    rows_of = pl.BlockSpec((steps, 64, 2 * DIM), lambda i: (i, 0, 0))
+    wide_heads = pl.BlockSpec((2 * tile, HEADS * DIM), lambda i: (i, 0))
     keep, send = pl.pallas_call(
         maps_kernel,
-        grid=(steps,),
-        in_specs=[scalar, piece, heads, heads, tile_rows],
+        grid=(2,),
+        in_specs=[scalar, piece, wide_heads, wide_heads, pl.BlockSpec((8, 2 * tile), lambda i: (0, i))],
         out_specs=[rows_of, rows_of],
         out_shape=[sorted_rows] * 2,
-        scratch_shapes=[parts, pltpu.VMEM((tile, 2 * DIM), f32)],
+        scratch_shapes=[parts, pltpu.VMEM((2 * tile, 2 * DIM), f32)],
         compiler_params=params(MAPS),
         name="maps",
     )(core, got, inputs, cotangent, rows)

time: 94.6 us -> 93.4 us (0.987)
  other arithmetic: 2.81 us -> 1.76 us
  local copies, waits for them, and re-layouts: 4.54 us -> 3.57 us
    pallas_call x1, Pallas kernels: 4.34 us -> 6.74 us  [on_device(): pl.pallas_call(rest_kernel, grid=(steps,), in_specs=[piece, heads, heads,...]
    add x1, other arithmetic: 1.91 us -> 0.87 us  [on_device(): near = keep_near + lax.ppermute(send_near, 'core', swap)]
    all_to_all x1, waiting for transfers between devices: 6.66 us -> 7.7 us  [on_device(): got = lax.all_to_all(scanned, SEQ, 0, 0)]
    pallas_call x1, Pallas kernels: 1.69 us -> 0.65 us  [on_device(): pl.pallas_call(sum_kernel, out_shape=[shape(64, DIM)] * 2, compiler_param...]
    unnamed x22 -> x26, local copies, waits for them, and re-layouts: 4.54 us -> 3.57 us
  transfers between devices with their start and end apart: 5 -> 5, of which waited for: 5 -> 5; matrix products, arithmetic and copies ran while one was open for 2% -> 1% of each run, Pallas kernels for 16% -> 19%
where the time goes in v5:
time: 93.4 us; the launch traced here: 92.9 us
  starting transfers between devices  38.6 us (41%)
  Pallas kernels  25 us (27%)
  waiting for transfers between devices  23.1 us (25%)
  local copies, waits for them, and re-layouts  3.57 us (4%)
  other arithmetic  1.76 us (2%)
    all_to_all x1, starting transfers between devices, on_device(): got = lax.all_to_all(pieces.reshape(32, 9, 4, DIM), SEQ, 0, 0)  13.7 us
    all_to_all x1, waiting for transfers between devices, on_device(): reduced = lax.all_to_all(reduced, 'y', 0, 0)  11.2 us
    pallas_call x1, Pallas kernels, on_device(): pl.pallas_call(local_kernel, in_specs=[scalar] + [whole(*v.shape) for v i...  10.7 us
    all_to_all x1, starting transfers between devices, on_device(): got = lax.all_to_all(scanned, SEQ, 0, 0)  8.26 us
    all_to_all x1, waiting for transfers between devices, on_device(): got = lax.all_to_all(scanned, SEQ, 0, 0)  7.7 us
    all_to_all x1, starting transfers between devices, on_device(): reduced = lax.all_to_all(reduced, 'y', 0, 0)  6.83 us
    pallas_call x1, Pallas kernels, on_device(): pl.pallas_call(rest_kernel, grid=(steps,), in_specs=[piece, heads, heads,...  6.74 us
    ppermute x1, starting transfers between devices, on_device(): reduced = keep + near + lax.ppermute(send, 'core', swap)  6.41 us
  transfers between devices with their start and end apart: 5, of which 5 were waited for; matrix products, arithmetic and copies ran while one was open for 1% of the time, Pallas kernels for 19%

profile of v5, /device:TPU:1, one launch (start us, length us, event | category | flops | bytes accessed | tf_op | source)
XLA Modules:
  0.0 92.9 jit_solution(564571988393965721)
XLA Ops:
  0.6 0.0 copy-start.1
  0.6 0.0 copy-start
  0.7 0.0 copy-start.4
  0.7 0.0 copy-start.3
  0.7 0.0 copy-start.9
  0.7 4.4 %states.1 = (f32[16,2,9,4,128]{4,3,2,1,0:T(4,128)}, f32[8,1024]{1,0:T(8,128)}) custom-call(bf16[1024,512]{1,0:T(8,128)(2,1)} %x_ref.7, bf16[1024,512]{1,0:T(8,128)(2,1)} %dy_ref.7, bf16[1024,128]{1,0:T(8,128)(2,1)} %b_ref.5, bf16[1024,128]{1,0:T(8,128)(2,1)} %c_ref.5, f32[4,1024]{1,0:T(4,128)} %rate_ref.3), custom_call_target="tpu_custom_call" | custom-call | tf_op jit(solution)/shard_map/states/pallas_call | solution.py:261
  5.1 13.7 %all-to-all-start = ((f32[32,9,4,128]{3,2,1,0:T(4,128)}), f32[32,9,4,128]{3,2,1,0:T(4,128)S(1)}, u32[]{:S(2)}, u32[]{:S(2)}) async-start(f32[32,9,4,128]{3,2,1,0:T(4,128)} %bitcast.2), calls=%async_computation | async-start | bytes 1179648 | tf_op jit(solution)/shard_map/all_to_all | solution.py:271
  18.8 0.0 copy-done.1
  18.8 0.0 copy-done
  18.8 0.0 copy-done.4
  18.8 0.0 copy-done.3
  18.8 0.0 copy-done.9
  18.9 10.7 %local.1 = (f32[1024,512]{1,0:T(8,128)S(1)}, f32[8,64,256]{2,1,0:T(8,128)S(1)}, f32[8,64,256]{2,1,0:T(8,128)S(1)}, f32[8,8,128]{2,1,0:T(8,128)S(1)}) custom-call(s32[1]{0:T(128)} %bitcast.core_ref, bf16[1024,512]{1,0:T(8,128)(2,1)S(1)} %copy-done, bf16[1024,512]{1,0:T(8,128)(2,1)S(1)} %copy-done.1, bf16[1024,128]{1,0:T(8,128)(2,1)S(1)} %copy-done.3, ...), custom_call_target="tpu_custom_call" | custom-call | tf_op jit(solution)/shard_map/local/pallas_call | solution.py:276
  29.6 0.0 copy-start.5
  29.6 1.3 %copy-done.5 = f32[1024,512]{1,0:T(8,128)} copy-done((f32[1024,512]{1,0:T(8,128)}, f32[1024,512]{1,0:T(8,128)S(1)}, u32[]{:S(2)}) %copy-start.5) | copy-done | bytes 2097176
  30.9 0.0 copy-start.6
  30.9 0.8 copy-done.6
  31.7 0.0 copy-start.10
  31.7 0.6 copy-done.10
  32.3 0.0 copy-start.11
  32.3 0.8 copy-done.11
  33.1 0.0 copy-start.8
  33.1 1.0 %all-to-all-done.got_ref = f32[32,9,4,128]{3,2,1,0:T(4,128)S(1)} async-done(((f32[32,9,4,128]{3,2,1,0:T(4,128)}), f32[32,9,4,128]{3,2,1,0:T(4,128)S(1)}, u32[]{:S(2)}, u32[]{:S(2)}) %all-to-all-start) | async-done | bytes 589856 | tf_op jit(solution)/shard_map/all_to_all | solution.py:271
  34.1 0.0 copy-start.7
  34.1 0.9 scan.1
  35.0 8.3 %all-to-all-start.1 = ((f32[32,32,128]{2,1,0:T(8,128)}), f32[32,32,128]{2,1,0:T(8,128)S(1)}, u32[]{:S(2)}, u32[]{:S(2)}) async-start(f32[32,32,128]{2,1,0:T(8,128)} %scan.1), calls=%async_computation.1 | async-start | bytes 1048576 | tf_op jit(solution)/shard_map/all_to_all | solution.py:300
  43.3 3.4 %collective-permute-start = (f32[8,64,256]{2,1,0:T(8,128)}, f32[8,64,256]{2,1,0:T(8,128)S(1)}, u32[]{:S(2)}, u32[]{:S(2)}) collective-permute-start(f32[8,64,256]{2,1,0:T(8,128)} %copy-done.11), channel_id=1, source_target_pairs={{0,1},{1,0},{2,3},{3,2},{4,5},{5,4},{6,7},{7,6},{8,9},{9,8},{10,11... | collective-permute-start | bytes 1572872 | tf_op jit(solution)/shard_map/ppermute | solution.py:302
  46.7 1.7 %collective-permute-done = f32[8,64,256]{2,1,0:T(8,128)S(1)} collective-permute-done((f32[8,64,256]{2,1,0:T(8,128)}, f32[8,64,256]{2,1,0:T(8,128)S(1)}, u32[]{:S(2)}, u32[]{:S(2)}) %collective-permute-start) | collective-permute-done | bytes 524320 | tf_op jit(solution)/shard_map/ppermute | solution.py:302
  48.4 0.0 copy-done.7
  48.5 0.9 add.9
  49.3 7.7 %all-to-all-done.1.got_ref = f32[32,32,128]{2,1,0:T(8,128)S(1)} async-done(((f32[32,32,128]{2,1,0:T(8,128)}), f32[32,32,128]{2,1,0:T(8,128)S(1)}, u32[]{:S(2)}, u32[]{:S(2)}) %all-to-all-start.1) | async-done | bytes 524320 | tf_op jit(solution)/shard_map/all_to_all | solution.py:300
  57.0 0.0 copy-start.2
  57.0 0.0 copy-start.12
  57.0 0.0 copy-done.8
  57.0 1.6 %maps.1 = (f32[8,64,256]{2,1,0:T(8,128)S(1)}, f32[8,64,256]{2,1,0:T(8,128)S(1)}) custom-call(s32[1]{0:T(128)} %bitcast.core_ref, f32[32,32,128]{2,1,0:T(8,128)S(1)} %all-to-all-done.1.got_ref, bf16[1024,512]{1,0:T(8,128)(2,1)S(1)} %copy-done, bf16[1024,512]{1,0:T(8,128)(2,1)S(1)} %copy-done.1, f32[8,1024]{1,0:T(8,128)S(1)} %copy-done.8), custom_call_target="tpu_custom_call" | custom-call | tf_op jit(solution)/shard_map/maps/pallas_call | solution.py:313
  58.7 6.4 %collective-permute-start.1 = (f32[8,64,256]{2,1,0:T(8,128)S(1)}, f32[8,64,256]{2,1,0:T(8,128)S(1)}, u32[]{:S(2)}, u32[]{:S(2)}) collective-permute-start(f32[8,64,256]{2,1,0:T(8,128)S(1)} %get-tuple-element.37), channel_id=1, source_target_pairs={{0,1},{1,0},{2,3},{3,2},{4,5},{5,4},{6,7},{7,6},{8,9},{9,8},{10,11... | collective-permute-start | bytes 1572872 | tf_op jit(solution)/shard_map/ppermute | solution.py:323
  65.1 1.5 %collective-permute-done.1 = f32[8,64,256]{2,1,0:T(8,128)S(1)} collective-permute-done((f32[8,64,256]{2,1,0:T(8,128)S(1)}, f32[8,64,256]{2,1,0:T(8,128)S(1)}, u32[]{:S(2)}, u32[]{:S(2)}) %collective-permute-start.1) | collective-permute-done | bytes 524320 | tf_op jit(solution)/shard_map/ppermute | solution.py:323
  66.6 0.0 copy-done.12
  66.6 0.9 add_add_fusion
  67.5 0.0 copy-done.2
  67.5 6.8 %all-to-all-start.2 = ((f32[8,64,256]{2,1,0:T(8,128)}), f32[8,64,256]{2,1,0:T(8,128)S(1)}, u32[]{:S(2)}, u32[]{:S(2)}) async-start(f32[8,64,256]{2,1,0:T(8,128)} %add_add_fusion), calls=%async_computation.2 | async-start | bytes 1048576 | tf_op jit(solution)/shard_map/all_to_all | solution.py:325
  74.3 6.7 %rest.1 = (f32[1024,512]{1,0:T(8,128)}, f32[4,1024]{1,0:T(4,128)}) custom-call(f32[32,32,128]{2,1,0:T(8,128)} %copy-done.2, bf16[1024,512]{1,0:T(8,128)(2,1)} %x_ref.7, bf16[1024,512]{1,0:T(8,128)(2,1)} %dy_ref.7, bf16[1024,128]{1,0:T(8,128)(2,1)} %b_ref.5, bf16[1024,128]{1,0:T(8,128)(2,1)} %c_ref.5, f32[8,1024]{1,0:T(8,128)} %get-tuple-element.34.rows_ref.tile_rows_ref, ...), custom_call_target="tpu_custom_call" | custom-call | tf_op jit(solution)/shard_map/rest/pallas_call | solution.py:326
  81.1 11.2 %all-to-all-done.2.parts_ref = f32[8,64,256]{2,1,0:T(8,128)S(1)} async-done(((f32[8,64,256]{2,1,0:T(8,128)}), f32[8,64,256]{2,1,0:T(8,128)S(1)}, u32[]{:S(2)}, u32[]{:S(2)}) %all-to-all-start.2) | async-done | bytes 524320 | tf_op jit(solution)/shard_map/all_to_all | solution.py:325
  92.3 0.7 sum.1
Async XLA Ops:
  0.6 18.2 %copy-start.1 = (bf16[1024,512]{1,0:T(8,128)(2,1)S(1)}, bf16[1024,512]{1,0:T(8,128)(2,1)}, u32[]{:S(2)}) copy-start(bf16[1024,512]{1,0:T(8,128)(2,1)} %dy_ref.7) | copy-start | bytes 3145732
  0.6 18.2 %copy-start = (bf16[1024,512]{1,0:T(8,128)(2,1)S(1)}, bf16[1024,512]{1,0:T(8,128)(2,1)}, u32[]{:S(2)}) copy-start(bf16[1024,512]{1,0:T(8,128)(2,1)} %x_ref.7) | copy-start | bytes 3145732
  0.7 18.2 %copy-start.4 = (bf16[1024,128]{1,0:T(8,128)(2,1)S(1)}, bf16[1024,128]{1,0:T(8,128)(2,1)}, u32[]{:S(2)}) copy-start(bf16[1024,128]{1,0:T(8,128)(2,1)} %c_ref.5) | copy-start | bytes 786436
  0.7 18.2 %copy-start.3 = (bf16[1024,128]{1,0:T(8,128)(2,1)S(1)}, bf16[1024,128]{1,0:T(8,128)(2,1)}, u32[]{:S(2)}) copy-start(bf16[1024,128]{1,0:T(8,128)(2,1)} %b_ref.5) | copy-start | bytes 786436
  0.7 18.2 %copy-start.9 = (f32[4,1024]{1,0:T(4,128)S(1)}, f32[4,1024]{1,0:T(4,128)}, u32[]{:S(2)}) copy-start(f32[4,1024]{1,0:T(4,128)} %rate_ref.3) | copy-start | bytes 49156
  5.1 29.0 %all-to-all-start = ((f32[32,9,4,128]{3,2,1,0:T(4,128)}), f32[32,9,4,128]{3,2,1,0:T(4,128)S(1)}, u32[]{:S(2)}, u32[]{:S(2)}) async-start(f32[32,9,4,128]{3,2,1,0:T(4,128)} %bitcast.2), calls=%async_computation | async-start | bytes 1179648 | tf_op jit(solution)/shard_map/all_to_all | solution.py:271
  29.6 1.3 %copy-start.5 = (f32[1024,512]{1,0:T(8,128)}, f32[1024,512]{1,0:T(8,128)S(1)}, u32[]{:S(2)}) copy-start(f32[1024,512]{1,0:T(8,128)S(1)} %get-tuple-element.39.gx0_ref) | copy-start | bytes 6291460
  30.9 0.8 copy-start.6
  31.7 0.6 copy-start.10
  32.3 0.8 copy-start.11
  33.1 23.9 %copy-start.8 = (f32[8,1024]{1,0:T(8,128)S(1)}, f32[8,1024]{1,0:T(8,128)}, u32[]{:S(2)}) copy-start(f32[8,1024]{1,0:T(8,128)} %get-tuple-element.34.rows_ref.tile_rows_ref) | copy-start | bytes 98308
  34.1 14.4 %copy-start.7 = (f32[8,64,256]{2,1,0:T(8,128)S(1)}, f32[8,64,256]{2,1,0:T(8,128)}, u32[]{:S(2)}) copy-start(f32[8,64,256]{2,1,0:T(8,128)} %copy-done.6) | copy-start | bytes 1572868
  35.0 22.0 %all-to-all-start.1 = ((f32[32,32,128]{2,1,0:T(8,128)}), f32[32,32,128]{2,1,0:T(8,128)S(1)}, u32[]{:S(2)}, u32[]{:S(2)}) async-start(f32[32,32,128]{2,1,0:T(8,128)} %scan.1), calls=%async_computation.1 | async-start | bytes 1048576 | tf_op jit(solution)/shard_map/all_to_all | solution.py:300
  43.3 5.2 %collective-permute-start = (f32[8,64,256]{2,1,0:T(8,128)}, f32[8,64,256]{2,1,0:T(8,128)S(1)}, u32[]{:S(2)}, u32[]{:S(2)}) collective-permute-start(f32[8,64,256]{2,1,0:T(8,128)} %copy-done.11), channel_id=1, source_target_pairs={{0,1},{1,0},{2,3},{3,2},{4,5},{5,4},{6,7},{7,6},{8,9},{9,8},{10,11... | collective-permute-start | bytes 1572872 | tf_op jit(solution)/shard_map/ppermute | solution.py:302
  57.0 10.5 %copy-start.2 = (f32[32,32,128]{2,1,0:T(8,128)}, f32[32,32,128]{2,1,0:T(8,128)S(1)}, u32[]{:S(2)}) copy-start(f32[32,32,128]{2,1,0:T(8,128)S(1)} %all-to-all-done.1.got_ref) | copy-start | bytes 1572868
  57.0 9.6 %copy-start.12 = (f32[8,64,256]{2,1,0:T(8,128)S(1)}, f32[8,64,256]{2,1,0:T(8,128)}, u32[]{:S(2)}) copy-start(f32[8,64,256]{2,1,0:T(8,128)} %add.9) | copy-start | bytes 1572868
  58.7 7.9 %collective-permute-start.1 = (f32[8,64,256]{2,1,0:T(8,128)S(1)}, f32[8,64,256]{2,1,0:T(8,128)S(1)}, u32[]{:S(2)}, u32[]{:S(2)}) collective-permute-start(f32[8,64,256]{2,1,0:T(8,128)S(1)} %get-tuple-element.37), channel_id=1, source_target_pairs={{0,1},{1,0},{2,3},{3,2},{4,5},{5,4},{6,7},{7,6},{8,9},{9,8},{10,11... | collective-permute-start | bytes 1572872 | tf_op jit(solution)/shard_map/ppermute | solution.py:323
  67.5 24.8 %all-to-all-start.2 = ((f32[8,64,256]{2,1,0:T(8,128)}), f32[8,64,256]{2,1,0:T(8,128)S(1)}, u32[]{:S(2)}, u32[]{:S(2)}) async-start(f32[8,64,256]{2,1,0:T(8,128)} %add_add_fusion), calls=%async_computation.2 | async-start | bytes 1048576 | tf_op jit(solution)/shard_map/all_to_all | solution.py:325

commit v6 on v5

--- a/solution.py
+++ b/solution.py
@@ -50,8 +50,10 @@
         totals = jnp.broadcast_to(jnp.exp(prefix[:, TOK - 1 :]), (8, DIM))
         total[0] = totals
         total[1] = jnp.concatenate([totals[2:], totals[:2]], axis=0)
-        turned[0] = b_ref[...].astype(f32).T
-        turned[1] = c_ref[...].astype(f32).T
+        unit = lax.broadcasted_iota(jnp.int32, (DIM, DIM), 0) == lax.broadcasted_iota(jnp.int32, (DIM, DIM), 1)
+        unit = unit.astype(f32).astype(bf16)
+        turned[0] = dot(unit, b_ref[...], ((1,), (1,)))
+        turned[1] = dot(unit, c_ref[...], ((1,), (1,)))
 
     for k in range(16):
         piece_ref[k, 0, 8] = total[step, 0:4, :]
@@ -308,15 +310,15 @@
     one = pl.BlockSpec((tile, DIM), lambda i: (i, 0))
     piece = whole(32, 32, DIM)
     tile_rows = pl.BlockSpec((8, tile), lambda i: (0, i))
-    rows_of = pl.BlockSpec((steps, 64, 2 * DIM), lambda i: (i, 0, 0))
-    wide_heads = pl.BlockSpec((2 * tile, HEADS * DIM), lambda i: (i, 0))
+    rows_of = pl.BlockSpec((2 * steps, 64, 2 * DIM), lambda i: (i, 0, 0))
+    wide_heads = pl.BlockSpec((4 * tile, HEADS * DIM), lambda i: (i, 0))
     keep, send = pl.pallas_call(
         maps_kernel,
-        grid=(2,),
-        in_specs=[scalar, piece, wide_heads, wide_heads, pl.BlockSpec((8, 2 * tile), lambda i: (0, i))],
+        grid=(1,),
+        in_specs=[scalar, piece, wide_heads, wide_heads, pl.BlockSpec((8, 4 * tile), lambda i: (0, i))],
         out_specs=[rows_of, rows_of],
         out_shape=[sorted_rows] * 2,
-        scratch_shapes=[parts, pltpu.VMEM((2 * tile, 2 * DIM), f32)],
+        scratch_shapes=[parts, pltpu.VMEM((4 * tile, 2 * DIM), f32)],
         compiler_params=params(MAPS),
         name="maps",
     )(core, got, inputs, cotangent, rows)

time: 93.4 us -> 93.2 us (level)
  no operation moved by 1% of the time
where the time goes in v6:
time: 93.2 us; the launch traced here: 92.7 us
  starting transfers between devices  38.7 us (42%)
  Pallas kernels  24.7 us (27%)
  waiting for transfers between devices  23.2 us (25%)
  local copies, waits for them, and re-layouts  3.57 us (4%)
  other arithmetic  1.76 us (2%)
    all_to_all x1, starting transfers between devices, on_device(): got = lax.all_to_all(pieces.reshape(32, 9, 4, DIM), SEQ, 0, 0)  13.7 us
    all_to_all x1, waiting for transfers between devices, on_device(): reduced = lax.all_to_all(reduced, 'y', 0, 0)  11.2 us
    pallas_call x1, Pallas kernels, on_device(): pl.pallas_call(local_kernel, in_specs=[scalar] + [whole(*v.shape) for v i...  10.7 us
    all_to_all x1, starting transfers between devices, on_device(): got = lax.all_to_all(scanned, SEQ, 0, 0)  8.28 us
    all_to_all x1, waiting for transfers between devices, on_device(): got = lax.all_to_all(scanned, SEQ, 0, 0)  7.72 us
    all_to_all x1, starting transfers between devices, on_device(): reduced = lax.all_to_all(reduced, 'y', 0, 0)  6.82 us
    pallas_call x1, Pallas kernels, on_device(): pl.pallas_call(rest_kernel, grid=(steps,), in_specs=[piece, heads, heads,...  6.74 us
    ppermute x1, starting transfers between devices, on_device(): reduced = keep + near + lax.ppermute(send, 'core', swap)  6.43 us
  transfers between devices with their start and end apart: 5, of which 5 were waited for; matrix products, arithmetic and copies ran while one was open for 1% of the time, Pallas kernels for 19%

profile of v6, /device:TPU:1, one launch (start us, length us, event | category | flops | bytes accessed | tf_op | source)
XLA Modules:
  0.0 92.7 jit_solution(17679993460700203151)
XLA Ops:
  0.6 0.0 copy-start.1
  0.6 0.0 copy-start
  0.7 0.0 copy-start.4
  0.7 0.0 copy-start.3
  0.7 0.0 copy-start.9
  0.7 4.3 %states.1 = (f32[16,2,9,4,128]{4,3,2,1,0:T(4,128)}, f32[8,1024]{1,0:T(8,128)}) custom-call(bf16[1024,512]{1,0:T(8,128)(2,1)} %x_ref.7, bf16[1024,512]{1,0:T(8,128)(2,1)} %dy_ref.7, bf16[1024,128]{1,0:T(8,128)(2,1)} %b_ref.5, bf16[1024,128]{1,0:T(8,128)(2,1)} %c_ref.5, f32[4,1024]{1,0:T(4,128)} %rate_ref.3), custom_call_target="tpu_custom_call" | custom-call | tf_op jit(solution)/shard_map/states/pallas_call | solution.py:263
  5.0 13.7 %all-to-all-start = ((f32[32,9,4,128]{3,2,1,0:T(4,128)}), f32[32,9,4,128]{3,2,1,0:T(4,128)S(1)}, u32[]{:S(2)}, u32[]{:S(2)}) async-start(f32[32,9,4,128]{3,2,1,0:T(4,128)} %bitcast.2), calls=%async_computation | async-start | bytes 1179648 | tf_op jit(solution)/shard_map/all_to_all | solution.py:273
  18.7 0.0 copy-done.1
  18.8 0.0 copy-done
  18.8 0.0 copy-done.4
  18.8 0.0 copy-done.3
  18.8 0.0 copy-done.9
  18.8 10.7 %local.1 = (f32[1024,512]{1,0:T(8,128)S(1)}, f32[8,64,256]{2,1,0:T(8,128)S(1)}, f32[8,64,256]{2,1,0:T(8,128)S(1)}, f32[8,8,128]{2,1,0:T(8,128)S(1)}) custom-call(s32[1]{0:T(128)} %bitcast.core_ref, bf16[1024,512]{1,0:T(8,128)(2,1)S(1)} %copy-done, bf16[1024,512]{1,0:T(8,128)(2,1)S(1)} %copy-done.1, bf16[1024,128]{1,0:T(8,128)(2,1)S(1)} %copy-done.3, ...), custom_call_target="tpu_custom_call" | custom-call | tf_op jit(solution)/shard_map/local/pallas_call | solution.py:278
  29.5 0.0 copy-start.5
  29.5 1.3 %copy-done.5 = f32[1024,512]{1,0:T(8,128)} copy-done((f32[1024,512]{1,0:T(8,128)}, f32[1024,512]{1,0:T(8,128)S(1)}, u32[]{:S(2)}) %copy-start.5) | copy-done | bytes 2097176
  30.8 0.0 copy-start.6
  30.8 0.8 copy-done.6
  31.6 0.0 copy-start.10
  31.6 0.6 copy-done.10
  32.2 0.0 copy-start.11
  32.2 0.8 copy-done.11
  33.0 0.0 copy-start.8
  33.0 1.0 %all-to-all-done.got_ref = f32[32,9,4,128]{3,2,1,0:T(4,128)S(1)} async-done(((f32[32,9,4,128]{3,2,1,0:T(4,128)}), f32[32,9,4,128]{3,2,1,0:T(4,128)S(1)}, u32[]{:S(2)}, u32[]{:S(2)}) %all-to-all-start) | async-done | bytes 589856 | tf_op jit(solution)/shard_map/all_to_all | solution.py:273
  34.0 0.0 copy-start.7
  34.0 0.9 scan.1
  34.9 8.3 %all-to-all-start.1 = ((f32[32,32,128]{2,1,0:T(8,128)}), f32[32,32,128]{2,1,0:T(8,128)S(1)}, u32[]{:S(2)}, u32[]{:S(2)}) async-start(f32[32,32,128]{2,1,0:T(8,128)} %scan.1), calls=%async_computation.1 | async-start | bytes 1048576 | tf_op jit(solution)/shard_map/all_to_all | solution.py:302
  43.2 3.4 %collective-permute-start = (f32[8,64,256]{2,1,0:T(8,128)}, f32[8,64,256]{2,1,0:T(8,128)S(1)}, u32[]{:S(2)}, u32[]{:S(2)}) collective-permute-start(f32[8,64,256]{2,1,0:T(8,128)} %copy-done.11), channel_id=1, source_target_pairs={{0,1},{1,0},{2,3},{3,2},{4,5},{5,4},{6,7},{7,6},{8,9},{9,8},{10,11... | collective-permute-start | bytes 1572872 | tf_op jit(solution)/shard_map/ppermute | solution.py:304
  46.6 1.7 %collective-permute-done = f32[8,64,256]{2,1,0:T(8,128)S(1)} collective-permute-done((f32[8,64,256]{2,1,0:T(8,128)}, f32[8,64,256]{2,1,0:T(8,128)S(1)}, u32[]{:S(2)}, u32[]{:S(2)}) %collective-permute-start) | collective-permute-done | bytes 524320 | tf_op jit(solution)/shard_map/ppermute | solution.py:304
  48.4 0.0 copy-done.7
  48.4 0.9 add.9
  49.2 7.7 %all-to-all-done.1.got_ref = f32[32,32,128]{2,1,0:T(8,128)S(1)} async-done(((f32[32,32,128]{2,1,0:T(8,128)}), f32[32,32,128]{2,1,0:T(8,128)S(1)}, u32[]{:S(2)}, u32[]{:S(2)}) %all-to-all-start.1) | async-done | bytes 524320 | tf_op jit(solution)/shard_map/all_to_all | solution.py:302
  57.0 0.0 copy-start.2
  57.0 0.0 copy-start.12
  57.0 0.0 copy-done.8
  57.0 1.4 %maps.1 = (f32[8,64,256]{2,1,0:T(8,128)S(1)}, f32[8,64,256]{2,1,0:T(8,128)S(1)}) custom-call(s32[1]{0:T(128)} %bitcast.core_ref, f32[32,32,128]{2,1,0:T(8,128)S(1)} %all-to-all-done.1.got_ref, bf16[1024,512]{1,0:T(8,128)(2,1)S(1)} %copy-done, bf16[1024,512]{1,0:T(8,128)(2,1)S(1)} %copy-done.1, f32[8,1024]{1,0:T(8,128)S(1)} %copy-done.8), custom_call_target="tpu_custom_call" | custom-call | tf_op jit(solution)/shard_map/maps/pallas_call | solution.py:315
  58.4 6.4 %collective-permute-start.1 = (f32[8,64,256]{2,1,0:T(8,128)S(1)}, f32[8,64,256]{2,1,0:T(8,128)S(1)}, u32[]{:S(2)}, u32[]{:S(2)}) collective-permute-start(f32[8,64,256]{2,1,0:T(8,128)S(1)} %get-tuple-element.37), channel_id=1, source_target_pairs={{0,1},{1,0},{2,3},{3,2},{4,5},{5,4},{6,7},{7,6},{8,9},{9,8},{10,11... | collective-permute-start | bytes 1572872 | tf_op jit(solution)/shard_map/ppermute | solution.py:325
  64.8 1.5 %collective-permute-done.1 = f32[8,64,256]{2,1,0:T(8,128)S(1)} collective-permute-done((f32[8,64,256]{2,1,0:T(8,128)S(1)}, f32[8,64,256]{2,1,0:T(8,128)S(1)}, u32[]{:S(2)}, u32[]{:S(2)}) %collective-permute-start.1) | collective-permute-done | bytes 524320 | tf_op jit(solution)/shard_map/ppermute | solution.py:325
  66.3 0.0 copy-done.12
  66.3 0.9 add_add_fusion
  67.2 0.0 copy-done.2
  67.2 6.8 %all-to-all-start.2 = ((f32[8,64,256]{2,1,0:T(8,128)}), f32[8,64,256]{2,1,0:T(8,128)S(1)}, u32[]{:S(2)}, u32[]{:S(2)}) async-start(f32[8,64,256]{2,1,0:T(8,128)} %add_add_fusion), calls=%async_computation.2 | async-start | bytes 1048576 | tf_op jit(solution)/shard_map/all_to_all | solution.py:327
  74.1 6.7 %rest.1 = (f32[1024,512]{1,0:T(8,128)}, f32[4,1024]{1,0:T(4,128)}) custom-call(f32[32,32,128]{2,1,0:T(8,128)} %copy-done.2, bf16[1024,512]{1,0:T(8,128)(2,1)} %x_ref.7, bf16[1024,512]{1,0:T(8,128)(2,1)} %dy_ref.7, bf16[1024,128]{1,0:T(8,128)(2,1)} %b_ref.5, bf16[1024,128]{1,0:T(8,128)(2,1)} %c_ref.5, f32[8,1024]{1,0:T(8,128)} %get-tuple-element.34.rows_ref.tile_rows_ref, ...), custom_call_target="tpu_custom_call" | custom-call | tf_op jit(solution)/shard_map/rest/pallas_call | solution.py:328
  80.8 11.2 %all-to-all-done.2.parts_ref = f32[8,64,256]{2,1,0:T(8,128)S(1)} async-done(((f32[8,64,256]{2,1,0:T(8,128)}), f32[8,64,256]{2,1,0:T(8,128)S(1)}, u32[]{:S(2)}, u32[]{:S(2)}) %all-to-all-start.2) | async-done | bytes 524320 | tf_op jit(solution)/shard_map/all_to_all | solution.py:327
  92.0 0.7 sum.1
Async XLA Ops:
  0.6 18.1 %copy-start.1 = (bf16[1024,512]{1,0:T(8,128)(2,1)S(1)}, bf16[1024,512]{1,0:T(8,128)(2,1)}, u32[]{:S(2)}) copy-start(bf16[1024,512]{1,0:T(8,128)(2,1)} %dy_ref.7) | copy-start | bytes 3145732
  0.6 18.1 %copy-start = (bf16[1024,512]{1,0:T(8,128)(2,1)S(1)}, bf16[1024,512]{1,0:T(8,128)(2,1)}, u32[]{:S(2)}) copy-start(bf16[1024,512]{1,0:T(8,128)(2,1)} %x_ref.7) | copy-start | bytes 3145732
  0.7 18.1 %copy-start.4 = (bf16[1024,128]{1,0:T(8,128)(2,1)S(1)}, bf16[1024,128]{1,0:T(8,128)(2,1)}, u32[]{:S(2)}) copy-start(bf16[1024,128]{1,0:T(8,128)(2,1)} %c_ref.5) | copy-start | bytes 786436
  0.7 18.1 %copy-start.3 = (bf16[1024,128]{1,0:T(8,128)(2,1)S(1)}, bf16[1024,128]{1,0:T(8,128)(2,1)}, u32[]{:S(2)}) copy-start(bf16[1024,128]{1,0:T(8,128)(2,1)} %b_ref.5) | copy-start | bytes 786436
  0.7 18.1 %copy-start.9 = (f32[4,1024]{1,0:T(4,128)S(1)}, f32[4,1024]{1,0:T(4,128)}, u32[]{:S(2)}) copy-start(f32[4,1024]{1,0:T(4,128)} %rate_ref.3) | copy-start | bytes 49156
  5.0 29.0 %all-to-all-start = ((f32[32,9,4,128]{3,2,1,0:T(4,128)}), f32[32,9,4,128]{3,2,1,0:T(4,128)S(1)}, u32[]{:S(2)}, u32[]{:S(2)}) async-start(f32[32,9,4,128]{3,2,1,0:T(4,128)} %bitcast.2), calls=%async_computation | async-start | bytes 1179648 | tf_op jit(solution)/shard_map/all_to_all | solution.py:273
  29.5 1.3 %copy-start.5 = (f32[1024,512]{1,0:T(8,128)}, f32[1024,512]{1,0:T(8,128)S(1)}, u32[]{:S(2)}) copy-start(f32[1024,512]{1,0:T(8,128)S(1)} %get-tuple-element.39.gx0_ref) | copy-start | bytes 6291460
  30.8 0.8 copy-start.6
  31.6 0.6 copy-start.10
  32.2 0.8 copy-start.11
  33.0 23.9 %copy-start.8 = (f32[8,1024]{1,0:T(8,128)S(1)}, f32[8,1024]{1,0:T(8,128)}, u32[]{:S(2)}) copy-start(f32[8,1024]{1,0:T(8,128)} %get-tuple-element.34.rows_ref.tile_rows_ref) | copy-start | bytes 98308
  34.0 14.4 %copy-start.7 = (f32[8,64,256]{2,1,0:T(8,128)S(1)}, f32[8,64,256]{2,1,0:T(8,128)}, u32[]{:S(2)}) copy-start(f32[8,64,256]{2,1,0:T(8,128)} %copy-done.6) | copy-start | bytes 1572868
  34.9 22.0 %all-to-all-start.1 = ((f32[32,32,128]{2,1,0:T(8,128)}), f32[32,32,128]{2,1,0:T(8,128)S(1)}, u32[]{:S(2)}, u32[]{:S(2)}) async-start(f32[32,32,128]{2,1,0:T(8,128)} %scan.1), calls=%async_computation.1 | async-start | bytes 1048576 | tf_op jit(solution)/shard_map/all_to_all | solution.py:302
  43.2 5.1 %collective-permute-start = (f32[8,64,256]{2,1,0:T(8,128)}, f32[8,64,256]{2,1,0:T(8,128)S(1)}, u32[]{:S(2)}, u32[]{:S(2)}) collective-permute-start(f32[8,64,256]{2,1,0:T(8,128)} %copy-done.11), channel_id=1, source_target_pairs={{0,1},{1,0},{2,3},{3,2},{4,5},{5,4},{6,7},{7,6},{8,9},{9,8},{10,11... | collective-permute-start | bytes 1572872 | tf_op jit(solution)/shard_map/ppermute | solution.py:304
  57.0 10.3 %copy-start.2 = (f32[32,32,128]{2,1,0:T(8,128)}, f32[32,32,128]{2,1,0:T(8,128)S(1)}, u32[]{:S(2)}) copy-start(f32[32,32,128]{2,1,0:T(8,128)S(1)} %all-to-all-done.1.got_ref) | copy-start | bytes 1572868
  57.0 9.4 %copy-start.12 = (f32[8,64,256]{2,1,0:T(8,128)S(1)}, f32[8,64,256]{2,1,0:T(8,128)}, u32[]{:S(2)}) copy-start(f32[8,64,256]{2,1,0:T(8,128)} %add.9) | copy-start | bytes 1572868
  58.4 8.0 %collective-permute-start.1 = (f32[8,64,256]{2,1,0:T(8,128)S(1)}, f32[8,64,256]{2,1,0:T(8,128)S(1)}, u32[]{:S(2)}, u32[]{:S(2)}) collective-permute-start(f32[8,64,256]{2,1,0:T(8,128)S(1)} %get-tuple-element.37), channel_id=1, source_target_pairs={{0,1},{1,0},{2,3},{3,2},{4,5},{5,4},{6,7},{7,6},{8,9},{9,8},{10,11... | collective-permute-start | bytes 1572872 | tf_op jit(solution)/shard_map/ppermute | solution.py:325
  67.2 24.8 %all-to-all-start.2 = ((f32[8,64,256]{2,1,0:T(8,128)}), f32[8,64,256]{2,1,0:T(8,128)S(1)}, u32[]{:S(2)}, u32[]{:S(2)}) async-start(f32[8,64,256]{2,1,0:T(8,128)} %add_add_fusion), calls=%async_computation.2 | async-start | bytes 1048576 | tf_op jit(solution)/shard_map/all_to_all | solution.py:327
